TPU v7x, 32 devices: a whole 2x2x4 slice. The times are simulated.
32 devices in a mesh: depth: 8 (over z, y), rows: 4 (over x, core).
Axes of the slice: x: 2, y: 2, z: 4, core: 2. Of those that a mesh axis runs over, the one named last changes fastest.
Arguments:
- density: float32 [4, 256, 8192], P('rows', 'depth'), may hold values from 0.00078125 to 0.015625
- attenuation: float32 [4, 256, 8192], P('rows', 'depth'), may hold values from 0.00078125 to 0.015625
- measured: float32 [4, 4, 8192], P(None, 'rows'), may hold values from -3 to 3
- angle_ids: int32 [4], replicated, may hold values from 0 to 359
- sides: int32 [4], replicated, may hold values from 0 to 1, as said below
Outputs:
- grad_density: float32 [4, 256, 8192], P('rows', 'depth')
- grad_attenuation: float32 [4, 256, 8192], P('rows', 'depth')
Inputs may be any that keep to these rules, and one draw needn't show every extreme that they name: Half of the 4 views have sides 1.
All inputs are finite; a program needn't handle non-finite values.
Results may differ from a plain program's by a relative error of at most 0.0001.
Values sent between devices are 32-bit elements; how exact they have to be, the bound alone decides.
No kernel may reach another device: no remote copies, remote signals or barrier semaphores. Data moves between devices by JAX's collectives and lax.ppermute only.
A program may use at most 64 MiB of HBM per device.

v0:
```python
import jax
import jax.numpy as jnp
from jax import lax
from jax.sharding import PartitionSpec as P

ANGLES = 360


def entering(value, axis, join, neutral):
    count, mine = (lax.axis_size(axis), lax.axis_index(axis))
    pieces = lax.all_gather(value, axis)
    subtotal = jnp.full_like(value, 0) + jnp.asarray(neutral, value.dtype)

    def step(position, subtotal):
        longer = join(subtotal, pieces[position])
        return jnp.where(position < mine, longer, subtotal)

    return lax.fori_loop(0, count - 1, step, subtotal)


def with_halo(block, sides, width):
    for axis, dim in sides:
        count = lax.axis_size(axis)
        forward = [(i, i + 1) for i in range(count - 1)]
        backward = [(target, source) for source, target in forward]
        low = lax.ppermute(
            lax.slice_in_dim(block, block.shape[dim] - width, None, axis=dim), axis, forward
        )
        high = lax.ppermute(lax.slice_in_dim(block, 0, width, axis=dim), axis, backward)
        block = jnp.concatenate([low, block, high], axis=dim)
    return block


def tilt_angle(angle_ids):
    return 0.8 * jnp.sin(jnp.pi * (angle_ids.astype(jnp.float32) + 0.5) / ANGLES - jnp.pi / 2)


def shifted_pair(field):
    widths = [(0, 0)] * (field.ndim - 1)
    from_left = jnp.pad(field[..., :-1], widths + [(1, 0)])
    from_right = jnp.pad(field[..., 1:], widths + [(0, 1)])
    return (from_left, from_right)


def resample(field, tilting):
    from_left, from_right = shifted_pair(field)
    return (
        (1.0 - jnp.abs(tilting)) * field
        + jnp.maximum(tilting, 0.0) * from_left
        + jnp.maximum(-tilting, 0.0) * from_right
    )


def resample_back(field, tilting):
    from_left, from_right = shifted_pair(field)
    return (
        (1.0 - jnp.abs(tilting)) * field
        + jnp.maximum(tilting, 0.0) * from_right
        + jnp.maximum(-tilting, 0.0) * from_left
    )


def strict_cumsum(field):
    depth_cells = field.shape[2]
    row_ids = lax.broadcasted_iota(jnp.int32, (depth_cells, depth_cells), 0)
    col_ids = lax.broadcasted_iota(jnp.int32, (depth_cells, depth_cells), 1)
    strictly_lower = (row_ids > col_ids).astype(jnp.float32)
    return jnp.einsum("ij,vrjc->vric", strictly_lower, field, precision=lax.Precision.HIGHEST)


def combine_sum(earlier, later):
    return earlier + later


def prefix_total(slab_values):
    earlier = entering(slab_values, "depth", combine_sum, jnp.zeros_like(slab_values))
    overall = lax.psum(slab_values, "depth")
    return (earlier, overall)


def detector_blur(image):
    padded = with_halo(image, (("rows", 1),), 1)
    return 0.25 * padded[:, :-2] + 0.5 * padded[:, 1:-1] + 0.25 * padded[:, 2:]


def on_device(density, attenuation, measured, angle_ids, sides):
    grad_density = jnp.zeros(density.shape, jnp.float32)
    grad_attenuation = jnp.zeros(density.shape, jnp.float32)
    tilting = tilt_angle(angle_ids)[:, None, None, None]
    far_side = (sides == 1)[:, None, None, None]
    emission = resample(density[None], tilting)
    absorb = resample(attenuation[None], tilting)
    before_absorb = strict_cumsum(absorb)
    absorb_in, absorb_all = prefix_total(jnp.sum(absorb, axis=2))
    nearer_sum = absorb_in[:, :, None, :] + before_absorb
    depth_sum = jnp.where(far_side, absorb_all[:, :, None, :] - nearer_sum - absorb, nearer_sum)
    transmit = jnp.exp(-depth_sum)
    radiance = emission * transmit
    before_radiance = strict_cumsum(radiance)
    radiance_in, signal = prefix_total(jnp.sum(radiance, axis=2))
    residual = detector_blur(signal) - measured
    back_signal = detector_blur(residual)[:, :, None, :]
    emitted_before = radiance_in[:, :, None, :] + before_radiance
    behind = jnp.where(far_side, emitted_before, signal[:, :, None, :] - emitted_before - radiance)
    grad_density = grad_density + jnp.sum(resample_back(back_signal * transmit, tilting), axis=0)
    grad_attenuation = grad_attenuation + jnp.sum(
        resample_back(-back_signal * behind, tilting), axis=0
    )
    return (grad_density, grad_attenuation)


def solution(mesh):
    placed = (P("rows", "depth", None), P("rows", "depth", None), P(None, "rows", None), P(), P())
    return jax.shard_map(
        on_device,
        mesh=mesh,
        in_specs=placed,
        out_specs=(P("rows", "depth", None), P("rows", "depth", None)),
        check_vma=False,
    )
```

profile of v0, /device:TPU:1, one launch (start us, length us, event | category | flops | bytes accessed | tf_op | source)
XLA Modules:
  0.0 301.4 jit_solution(13441340693976916239)
XLA Ops:
  7.9 2.0 fusion.29
  10.3 1.0 copy-done.3
  11.2 1.8 fusion.10
  13.0 1.6 fusion.28
  14.7 3.2 %pad_bitcast_fusion.2 = (f32[32,8192]{1,0:T(8,128)}, f32[32,8192]{1,0:T(8,128)}) fusion(f32[1,1,32,8191]{3,2,1,0:T(8,128)} %get-tuple-element.227, f32[1,1,32,8191]{3,2,1,0:T(8,128)} %get-tuple-element.226), kind=kLoop, calls=%fused_computation.36 | loop fusion | bytes 4194048 | tf_op jit(solution)/shard_map/mul | solution.py:50
  17.9 35.9 %all-gather.7.cloned.1.call-done = f32[8,4,8192]{2,1,0:T(4,128)} async-done(((f32[1,4,8192]{2,1,0:T(4,128)}), f32[8,4,8192]{2,1,0:T(4,128)}) %all-gather.7.cloned.1.call-update) | async-done | bytes 1048592 | tf_op jit(solution)/shard_map/all_gather | solution.py:11
  54.6 8.0 %while.28 = (s32[]{:T(128)}, f32[4,1,8192]{2,1,0:T(1,128)S(1)}, s32[]{:T(128)}, f32[8,4,1,8192]{3,1,0,2:T(4,128)}, s32[]{:T(128)}, /*index=5*/s32[]{:T(128)}) while((s32[]{:T(128)}, f32[4,1,8192]{2,1,0:T(1,128)S(1)}, s32[]{:T(128)}, f32[8,4,1,8192]{3,1,0,2:T(4,128)}, s32[]{:T(128)}, /*index=5*/s32[]{:T(128)}) %tuple.91), condition=%wide.region_3.4_spmd.clone, body=%wide.region_2.3_spmd.clone.sunk | while | flops 98308 | bytes 655461 | solution.py:18
  54.6 0.9 constant_dynamic-slice_fusion.4
  55.8 0.9 constant_dynamic-slice_fusion.4
  56.9 0.9 constant_dynamic-slice_fusion.4
  58.1 0.9 constant_dynamic-slice_fusion.4
  59.2 0.9 constant_dynamic-slice_fusion.4
  60.4 0.9 constant_dynamic-slice_fusion.4
  61.5 0.9 constant_dynamic-slice_fusion.4
  62.7 64.2 %all-reduce.11.cloned.1.call-done = f32[4,8192]{1,0:T(4,128)} async-done(((f32[4,8192]{1,0:T(4,128)}), f32[4,8192]{1,0:T(4,128)}) %all-reduce.11.cloned.1.call-update) | async-done | bytes 131088 | tf_op jit(solution)/shard_map/psum | solution.py:77
  127.0 9.0 %fusion.24 = (f32[4,8192]{1,0:T(4,128)}, f32[4,1,32,8192]{3,2,0,1:T(8,128)}) fusion(f32[32,8192]{1,0:T(8,128)} %get-tuple-element.234, f32[4]{0:T(128)S(1)} %get-tuple-element.231, f32[32,8192]{1,0:T(8,128)} %get-tuple-element.235, f32[4]{0:T(128)S(1)} %get-tuple-element.230, f32[32,8192]{1,0:T(8,128)S(1)} %bitcast.82, f32[4]{0:T(128)S(1)} %get-tuple-element.220, ...), kind=kOutput, calls=%fused_computation.49 | convolution fusion | flops 425690112 | bytes 10879028 | tf_op jit(solution)/shard_map/ij,vrjc->vric/dot_general | solution.py:68
  136.0 39.7 %all-gather.9.cloned.1.call-done = f32[8,4,8192]{2,1,0:T(4,128)} async-done(((f32[1,4,8192]{2,1,0:T(4,128)}), f32[8,4,8192]{2,1,0:T(4,128)}) %all-gather.9.cloned.1.call-update) | async-done | bytes 1048592 | tf_op jit(solution)/shard_map/all_gather | solution.py:11
  176.2 72.8 %all-reduce.13.cloned.1.call-done = f32[4,1,8192]{2,0,1:T(4,128)} async-done(((f32[4,1,8192]{2,0,1:T(4,128)}), f32[4,1,8192]{2,0,1:T(4,128)}) %all-reduce.13.cloned.1.call-update) | async-done | bytes 131088 | tf_op jit(solution)/shard_map/psum | solution.py:77
  249.1 4.4 %collective-permute-start.1 = (f32[4,1,8192]{2,0,1:T(4,128)}, f32[4,1,8192]{2,0,1:T(4,128)S(1)}, u32[]{:S(2)}, u32[]{:S(2)}) collective-permute-start(f32[4,1,8192]{2,0,1:T(4,128)} %all-reduce.13.cloned.1.call-done), channel_id=1, source_target_pairs={{1,0},{2,1},{3,2},{5,4},{6,5},{7,6},{9,8},{10,9},{11,10},{13,12},{... | collective-permute-start | bytes 393224 | tf_op jit(solution)/shard_map/ppermute | solution.py:29
  253.5 3.0 collective-permute-start
  257.4 1.3 collective-permute-done
  258.8 1.0 copy_subtract_fusion
  259.8 1.9 collective-permute-start.3
  261.7 4.4 %collective-permute-start.2 = (f32[4,1,8192]{2,0,1:T(4,128)S(1)}, f32[4,1,8192]{2,0,1:T(4,128)S(1)}, u32[]{:S(2)}, u32[]{:S(2)}) collective-permute-start(f32[4,1,8192]{2,0,1:T(4,128)S(1)} %copy_subtract_fusion), channel_id=1, source_target_pairs={{0,1},{1,2},{2,3},{4,5},{5,6},{6,7},{8,9},{9,10},{10,11},{12,13},{... | collective-permute-start | bytes 393224 | tf_op jit(solution)/shard_map/ppermute | solution.py:26
  266.2 8.0 %while.29 = (s32[]{:T(128)}, f32[4,1,8192]{2,1,0:T(1,128)S(1)}, s32[]{:T(128)}, f32[8,4,1,8192]{3,1,0,2:T(4,128)}, s32[]{:T(128)}, /*index=5*/s32[]{:T(128)}) while((s32[]{:T(128)}, f32[4,1,8192]{2,1,0:T(1,128)S(1)}, s32[]{:T(128)}, f32[8,4,1,8192]{3,1,0,2:T(4,128)}, s32[]{:T(128)}, /*index=5*/s32[]{:T(128)}) %tuple.90), condition=%wide.region_8.9_spmd.clone, body=%wide.region_7.8_spmd.clone.sunk | while | flops 98308 | bytes 655461 | solution.py:18
  270.8 0.9 constant_dynamic-slice_fusion.5
  271.9 0.9 constant_dynamic-slice_fusion.5
  274.4 2.6 broadcast_multiply_fusion
  277.1 1.5 fusion.26
  279.8 5.0 %select_multiply_fusion = f32[4,1,32,8192]{3,2,0,1:T(8,128)S(1)} fusion(f32[4,8192]{1,0:T(4,128)S(1)} %bitcast.91, f32[4,8192]{1,0:T(4,128)S(1)} %get-tuple-element.218, pred[4]{0:T(512)(128)(4,1)S(1)} %broadcast_compare_fusion, f32[4,8192]{1,0:T(4,128)S(1)} %bitcast.92, f32[4,1,32,8192]{3,2,0,1:T(8,128)S(1)} %copy-done, f32[32,8192]{1,0:T(8,128)S(1)} %copy-done.4, ...), kind=kOutput, calls=%fused_computation.16 | convolution fusion | flops 420480000 | bytes 11927604 | tf_op jit(solution)/shard_map/ij,vrjc->vric/dot_general | solution.py:68
  284.8 3.5 %fusion.27 = (f32[4,1,32,8191]{3,2,0,1:T(8,128)S(1)}, f32[4,1,32,8191]{3,2,0,1:T(8,128)}) fusion(f32[4,1,32,8192]{3,2,0,1:T(8,128)S(1)} %select_multiply_fusion), kind=kLoop, calls=%fused_computation.52 | loop fusion | bytes 16775168 | tf_op jit(solution)/shard_map/slice | solution.py:41
  288.3 6.5 %add_reduce_fusion = (f32[32,8192]{1,0:T(8,128)}, f32[32,8192]{1,0:T(8,128)}) fusion(f32[4,1,32,8191]{3,2,0,1:T(8,128)} %get-tuple-element.225, f32[4,1,32,8191]{3,2,0,1:T(8,128)S(1)} %get-tuple-element.224, f32[4,1,32,8192]{3,2,0,1:T(8,128)S(1)} %select_multiply_fusion, f32[4]{0:T(128)S(1)} %get-tuple-element.231, f32[4]{0:T(128)S(1)} %get-tuple-element.230, ...), kind=kLoop, calls=%fused_computation.15 | loop fusion | flops 13107200 | bytes 27392048 | tf_op jit(solution)/shard_map/reduce_sum | solution.py:106
  (56 shorter events, 12.3 us)
Async XLA Ops:
  7.2 46.7 %all-gather.7.cloned.1.call-start = ((), (), s32[]{:S(2)}) async-start(), calls=%async_computation.2 | async-start | bytes 1179648 | tf_op jit(solution)/shard_map/all_gather | solution.py:11
  7.9 3.3 %copy-start.1 = (f32[1,32,8192]{2,1,0:T(8,128)S(1)}, f32[1,32,8192]{2,1,0:T(8,128)}, u32[]{:S(2)}) copy-start(f32[1,32,8192]{2,1,0:T(8,128)} %param.10) | copy-start | bytes 3145732
  9.9 3.1 %copy-start.2 = (f32[1,32,8192]{2,1,0:T(8,128)S(1)}, f32[1,32,8192]{2,1,0:T(8,128)}, u32[]{:S(2)}) copy-start(f32[1,32,8192]{2,1,0:T(8,128)} %param.9) | copy-start | bytes 3145732
  10.3 1.0 copy-start.3
  10.3 4.4 %copy-start.8 = (s32[4]{0:T(128)S(1)}, s32[4]{0:T(128)}, u32[]{:S(2)}) copy-start(s32[4]{0:T(128)} %param.13) | copy-start | bytes 52
  53.8 73.1 %all-reduce.11.cloned.1.call-start = ((), (), s32[]{:S(2)}) async-start(), calls=%async_computation | async-start | bytes 262144 | tf_op jit(solution)/shard_map/psum | solution.py:77
  54.6 121.1 %all-gather.9.cloned.1.call-start = ((), (), s32[]{:S(2)}) async-start(), calls=%async_computation.3 | async-start | bytes 1179648 | tf_op jit(solution)/shard_map/all_gather | solution.py:11
  127.0 131.8 %copy-start.6 = (f32[4,1,8192]{2,1,0:T(1,128)S(1)}, f32[4,1,8192]{2,1,0:T(1,128)}, u32[]{:S(2)}) copy-start(f32[4,1,8192]{2,1,0:T(1,128)} %param.11) | copy-start | bytes 393220
  175.7 73.4 %all-reduce.13.cloned.1.call-start = ((), (), s32[]{:S(2)}) async-start(), calls=%async_computation.1 | async-start | bytes 262144 | tf_op jit(solution)/shard_map/psum | solution.py:77
  249.1 8.4 %collective-permute-start.1 = (f32[4,1,8192]{2,0,1:T(4,128)}, f32[4,1,8192]{2,0,1:T(4,128)S(1)}, u32[]{:S(2)}, u32[]{:S(2)}) collective-permute-start(f32[4,1,8192]{2,0,1:T(4,128)} %all-reduce.13.cloned.1.call-done), channel_id=1, source_target_pairs={{1,0},{2,1},{3,2},{5,4},{6,5},{7,6},{9,8},{10,9},{11,10},{13,12},{... | collective-permute-start | bytes 393224 | tf_op jit(solution)/shard_map/ppermute | solution.py:29
  253.5 5.2 %collective-permute-start = (f32[4,1,8192]{2,0,1:T(4,128)}, f32[4,1,8192]{2,0,1:T(4,128)S(1)}, u32[]{:S(2)}, u32[]{:S(2)}) collective-permute-start(f32[4,1,8192]{2,0,1:T(4,128)} %all-reduce.13.cloned.1.call-done), channel_id=1, source_target_pairs={{0,1},{1,2},{2,3},{4,5},{5,6},{6,7},{8,9},{9,10},{10,11},{12,13},{... | collective-permute-start | bytes 393224 | tf_op jit(solution)/shard_map/ppermute | solution.py:26
  259.8 14.5 %collective-permute-start.3 = (f32[4,1,8192]{2,0,1:T(4,128)S(1)}, f32[4,1,8192]{2,0,1:T(4,128)S(1)}, u32[]{:S(2)}, u32[]{:S(2)}) collective-permute-start(f32[4,1,8192]{2,0,1:T(4,128)S(1)} %copy_subtract_fusion), channel_id=1, source_target_pairs={{1,0},{2,1},{3,2},{5,4},{6,5},{7,6},{9,8},{10,9},{11,10},{13,12},{... | collective-permute-start | bytes 393224 | tf_op jit(solution)/shard_map/ppermute | solution.py:29
  261.7 12.6 %collective-permute-start.2 = (f32[4,1,8192]{2,0,1:T(4,128)S(1)}, f32[4,1,8192]{2,0,1:T(4,128)S(1)}, u32[]{:S(2)}, u32[]{:S(2)}) collective-permute-start(f32[4,1,8192]{2,0,1:T(4,128)S(1)} %copy_subtract_fusion), channel_id=1, source_target_pairs={{0,1},{1,2},{2,3},{4,5},{5,6},{6,7},{8,9},{9,10},{10,11},{12,13},{... | collective-permute-start | bytes 393224 | tf_op jit(solution)/shard_map/ppermute | solution.py:26
  277.0 2.2 copy-start
  277.0 2.5 copy-start.4
  277.1 2.8 copy-start.5
  277.1 2.8 copy-start.7
Sparse Core Ops, SparseCore 0:
  13.1 40.6 all-gather.6
  58.0 68.9 all-reduce.10
  136.1 39.5 all-gather.8
  180.1 68.9 all-reduce.12
where the time goes:
time: 302 us; the launch traced here: 301 us
  waiting for transfers between devices  216 us (72%)
  local copies, waits for them, and re-layouts  27.4 us (9%)
  other arithmetic  15.5 us (5%)
  matrix products  14 us (5%)
  between operations  14 us (5%)
  starting transfers between devices  13.9 us (5%)
    psum x2, waiting for transfers between devices, prefix_total(): overall = lax.psum(slab_values, 'depth')  137 us
    all_gather x2, waiting for transfers between devices, entering(): pieces = lax.all_gather(value, axis)  75.6 us
    dot_general x2, matrix products, strict_cumsum(): jnp.einsum('ij,vrjc->vric', strictly_lower, field, precision=lax.Precisio...  14 us
    dynamic_slice x14, local copies, waits for them, and re-layouts, step(): longer = join(subtotal, pieces[position])  12.8 us
    ppermute x2, starting transfers between devices, with_halo(): lax.ppermute(lax.slice_in_dim(block, block.shape[dim] - width, None, axis...  7.42 us
    reduce_sum x1, other arithmetic, on_device(): jnp.sum(resample_back(-back_signal * behind, tilting), axis=0)  6.54 us
    ppermute x2, starting transfers between devices, with_halo(): lax.ppermute(lax.slice_in_dim(block, 0, width, axis=dim), axis, backward)  6.35 us
  transfers between devices with their start and end apart: 8, of which 6 were waited for; matrix products, arithmetic and copies ran while one was open for 7% of the time, Pallas kernels for 0%

commit v1 on v0

v1 whole, which is shorter than its diff:
```python
import functools
import math

import jax
import jax.numpy as jnp
from jax import lax
from jax.experimental import pallas as pl
from jax.experimental.pallas import tpu as pltpu
from jax.sharding import PartitionSpec as P

ANGLES = 360
PAD = 128
F32 = jnp.float32
BF16 = jnp.bfloat16


def tilt_parts(angle):
    tilt = 0.8 * jnp.sin(jnp.pi * (angle.astype(F32) + 0.5) / ANGLES - jnp.pi / 2)
    return 1.0 - jnp.abs(tilt), jnp.maximum(tilt, 0.0), jnp.maximum(-tilt, 0.0)


def view_column(ref, views, shape):
    rows = lax.broadcasted_iota(jnp.int32, shape, 0)
    out = jnp.full(shape, ref[0], jnp.int32)
    for v in range(1, views):
        out = jnp.where(rows == v, ref[v], out)
    return out


def strict_sums(rows, cells, first):
    i = lax.broadcasted_iota(jnp.int32, (rows, 2 * cells), 0)
    j = lax.broadcasted_iota(jnp.int32, (rows, 2 * cells), 1)
    j = jnp.where(j >= cells, j - cells, j)
    below = jnp.where(first, (j < i).astype(jnp.int32), (j > i).astype(jnp.int32))
    return jnp.where(i >= cells, 1, below).astype(F32).astype(BF16)


def two_terms(value):
    high = value.astype(BF16)
    low = (value - high.astype(F32)).astype(BF16)
    return jnp.concatenate([high, low], axis=0)


def neighbours(block):
    width = block.shape[-1]
    inner = slice(PAD, width - PAD)
    return pltpu.roll(block, 1, 1)[:, inner], pltpu.roll(block, width - 1, 1)[:, inner]


def slab_kernel(views, wide, angle_ref, side_ref, place_ref, d_ref, a_ref, m_ref, up_ref, lt_ref, lb_ref, x_ref, t_ref, e_ref):
    cells, columns = d_ref.shape
    chunks = columns // wide
    lower = strict_sums(cells + 8, cells, True)
    upper = strict_sums(cells + 8, cells, False)
    for ref in (x_ref, e_ref):
        for edge in (0, PAD + columns):
            ref[..., pl.ds(edge, PAD)] = jnp.zeros(ref.shape[:-1] + (PAD,), F32)
    for edge in (0, PAD + columns):
        t_ref[:, pl.ds(edge, PAD)] = jnp.zeros((8, PAD), F32)

    def sums(j, carry):
        at = pl.multiple_of(j * wide, PAD)
        into = pl.ds(pl.multiple_of(at + PAD, PAD), wide)
        terms = two_terms(a_ref[:, pl.ds(at, wide)])
        below = jnp.dot(lower, terms, preferred_element_type=F32)
        above = jnp.dot(upper, terms, preferred_element_type=F32)
        x_ref[0, 0, :, into] = below[:cells]
        x_ref[0, 1, :, into] = above[:cells]
        t_ref[:, into] = below[cells:]
        e_ref[0, :, into] = d_ref[:, pl.ds(at, wide)]
        return carry

    lax.fori_loop(0, chunks, sums, 0)

    def shifts(j, carry):
        at = pl.multiple_of(j * wide, PAD)
        around = pl.ds(at, wide + 2 * PAD)
        into = pl.ds(pl.multiple_of(at + PAD, PAD), wide)
        for side in range(2):
            left, right = neighbours(x_ref[0, side, :, around])
            x_ref[1, side, :, into] = left
            x_ref[2, side, :, into] = right
        left, right = neighbours(e_ref[0, :, around])
        e_ref[1, :, into] = left
        e_ref[2, :, into] = right
        return carry

    lax.fori_loop(0, chunks, shifts, 0)

    centres, besides, behind_sums = [], [], []
    for v in range(views):
        centre, left, right = tilt_parts(jnp.full((8, 128), angle_ref[v], jnp.int32))
        centres.append(centre[:1, :1])
        besides.append((left + right)[:1, :1])
        behind_sums.append(jnp.where(side_ref[v] == 1, lower.astype(F32), upper.astype(F32)).astype(BF16))
    place = lax.rem(place_ref[0], views)

    def rays(j, carry):
        at = pl.multiple_of(j * wide, PAD)
        into = pl.ds(pl.multiple_of(at + PAD, PAD), wide)
        rows = []
        for v in range(views):
            shift = jnp.where(angle_ref[v] * 2 >= ANGLES, 1, 2)
            depth = centres[v] * x_ref[0, side_ref[v], :, into] + besides[v] * x_ref[shift, side_ref[v], :, into]
            light = jnp.exp(-depth)
            emission = centres[v] * e_ref[0, :, into] + besides[v] * e_ref[shift, :, into]
            behind = jnp.dot(behind_sums[v], two_terms(emission * light), preferred_element_type=F32)
            lt_ref[v, :, pl.ds(at, wide)] = light
            lb_ref[v, :, pl.ds(at, wide)] = behind[:cells]
            rows.append(behind[cells : cells + 1])
        left, right = neighbours(t_ref[:, pl.ds(at, wide + 2 * PAD)])
        rows += [left[:1], t_ref[:1, into], right[:1], m_ref[pl.ds(place, 1), pl.ds(at, wide)]]
        up_ref[j] = jnp.concatenate(rows, axis=0)
        return carry

    lax.fori_loop(0, chunks, rays, 0)


def column_kernel(views, slabs, rows, angle_ref, side_ref, up_ref, down_ref):
    wide = up_ref.shape[-1]
    shape = (views, wide)
    centre, left, right = tilt_parts(view_column(angle_ref, views, shape))
    far = view_column(side_ref, views, shape) == 1
    passes, behinds, signals = {}, {}, []
    for r in range(rows):
        absorbs, runs = [], []
        run = jnp.zeros(shape, F32)
        for k in range(slabs):
            block = up_ref[k * rows + r]
            absorb = left * block[views : views + 1] + centre * block[views + 1 : views + 2] + right * block[views + 2 : views + 3]
            runs.append(run)
            absorbs.append(absorb)
            run = run + absorb
        radiances, starts = [], []
        signal = jnp.zeros(shape, F32)
        for k in range(slabs):
            entering = jnp.where(far, run - runs[k] - absorbs[k], runs[k])
            passes[k, r] = jnp.exp(-entering)
            radiance = passes[k, r] * up_ref[k * rows + r][:views]
            starts.append(signal)
            radiances.append(radiance)
            signal = signal + radiance
        for k in range(slabs):
            behinds[k, r] = jnp.where(far, starts[k], signal - starts[k] - radiances[k])
        signals.append(signal)

    def blur(values):
        out = []
        for r in range(rows):
            total = 0.5 * values[r]
            if r > 0:
                total = total + 0.25 * values[r - 1]
            if r + 1 < rows:
                total = total + 0.25 * values[r + 1]
            out.append(total)
        return out

    residuals = []
    for r, value in enumerate(blur(signals)):
        seen = jnp.concatenate([up_ref[v * rows + r][views + 3 : views + 4] for v in range(views)], axis=0)
        residuals.append(value - seen)
    for r, back in enumerate(blur(residuals)):
        for k in range(slabs):
            scaled = back * behinds[k, r]
            parts = [back * passes[k, r]]
            for weight in (centre, left, right):
                parts.append(jnp.sum(weight * scaled, axis=0, keepdims=True))
            parts.append(jnp.zeros((1, wide), F32))
            down_ref[k * rows + r] = jnp.concatenate(parts, axis=0)


def gradient_kernel(views, wide, angle_ref, down_ref, lt_ref, lb_ref, gd_ref, ga_ref, p_ref):
    cells, columns = gd_ref.shape
    chunks = columns // wide
    for edge in (0, PAD + columns):
        p_ref[..., pl.ds(edge, PAD)] = jnp.zeros(p_ref.shape[:-1] + (PAD,), F32)
    weights = []
    for v in range(views):
        weights.append([part[:1, :1] for part in tilt_parts(jnp.full((8, 128), angle_ref[v], jnp.int32))])

    def products(j, carry):
        at = pl.multiple_of(j * wide, PAD)
        into = pl.ds(pl.multiple_of(at + PAD, PAD), wide)
        block = down_ref[j]
        density = [None] * 3
        absorb = [jnp.broadcast_to(block[views + i : views + i + 1], (cells, wide)) for i in range(3)]
        for v in range(views):
            light = lt_ref[v, :, pl.ds(at, wide)]
            behind = lb_ref[v, :, pl.ds(at, wide)]
            for i in range(3):
                scale = weights[v][i] * block[v : v + 1]
                density[i] = scale * light if density[i] is None else density[i] + scale * light
                absorb[i] = absorb[i] + scale * behind
        for i in range(3):
            p_ref[0, i, :, into] = density[i]
            p_ref[1, i, :, into] = absorb[i]
        return carry

    lax.fori_loop(0, chunks, products, 0)

    def shifts(j, carry):
        at = pl.multiple_of(j * wide, PAD)
        around = pl.ds(at, wide + 2 * PAD)
        into = pl.ds(pl.multiple_of(at + PAD, PAD), wide)
        for q, (ref, sign) in enumerate(((gd_ref, 1.0), (ga_ref, -1.0))):
            after = neighbours(p_ref[q, 1, :, around])[1]
            before = neighbours(p_ref[q, 2, :, around])[0]
            ref[:, pl.ds(at, wide)] = sign * (p_ref[q, 0, :, into] + after + before)
        return carry

    lax.fori_loop(0, chunks, shifts, 0)


def on_device(density, attenuation, measured, angle_ids, sides):
    cells, columns = density.shape[1:]
    views = measured.shape[0]
    slabs, rows = lax.axis_size("depth"), lax.axis_size("rows")
    devices = slabs * rows
    part = columns // devices
    wide = part if part % PAD == 0 else 2 * PAD
    smem = pl.BlockSpec(memory_space=pltpu.SMEM)
    vmem = pl.BlockSpec(memory_space=pltpu.VMEM)
    place = lax.axis_index("depth").astype(jnp.int32)[None]
    padded = columns + 2 * PAD
    up, light, behind = pl.pallas_call(
        functools.partial(slab_kernel, views, wide),
        out_shape=(
            jax.ShapeDtypeStruct((columns // wide, views + 4, wide), F32),
            jax.ShapeDtypeStruct((views, cells, columns), F32),
            jax.ShapeDtypeStruct((views, cells, columns), F32),
        ),
        in_specs=[smem] * 3 + [vmem] * 3,
        out_specs=(vmem,) * 3,
        scratch_shapes=[
            pltpu.VMEM((3, 2, cells, padded), F32),
            pltpu.VMEM((8, padded), F32),
            pltpu.VMEM((3, cells, padded), F32),
        ],
        name="slab",
    )(angle_ids, sides, place, density[0], attenuation[0], measured[:, 0])

    def regroup(blocks, count, width):
        if blocks.shape[0] == count:
            return blocks
        flat = blocks.transpose(1, 0, 2).reshape(blocks.shape[1], columns)
        return flat.reshape(blocks.shape[1], count, width).transpose(1, 0, 2)

    up = lax.all_to_all(regroup(up, devices, part), ("depth", "rows"), 0, 0)
    down = pl.pallas_call(
        functools.partial(column_kernel, views, slabs, rows),
        out_shape=jax.ShapeDtypeStruct(up.shape, F32),
        in_specs=[smem] * 2 + [vmem],
        out_specs=vmem,
        name="column",
    )(angle_ids, sides, up)
    down = regroup(lax.all_to_all(down, ("depth", "rows"), 0, 0), columns // wide, wide)
    grads = pl.pallas_call(
        functools.partial(gradient_kernel, views, wide),
        out_shape=(jax.ShapeDtypeStruct((cells, columns), F32),) * 2,
        in_specs=[smem] + [vmem] * 3,
        out_specs=(vmem,) * 2,
        scratch_shapes=[pltpu.VMEM((2, 3, cells, padded), F32)],
        name="gradient",
    )(angle_ids, down, light, behind)
    return grads[0][None], grads[1][None]


def solution(mesh):
    placed = (P("rows", "depth", None), P("rows", "depth", None), P(None, "rows", None), P(), P())
    return jax.shard_map(
        on_device,
        mesh=mesh,
        in_specs=placed,
        out_specs=(P("rows", "depth", None), P("rows", "depth", None)),
        check_vma=False,
    )
```

time: 302 us -> 69.3 us (0.23)
  waiting for transfers between devices: 216 us -> 0 us
  Pallas kernels: 0 us -> 34.9 us
  blocking collectives: 0 us -> 31.3 us
  local copies, waits for them, and re-layouts: 27.4 us -> 1.65 us
  other arithmetic: 15.5 us -> 0 us
  matrix products: 14 us -> 0 us
  starting transfers between devices: 13.9 us -> 0 us
  between operations: 14 us -> 0.64 us
    psum x2 -> x0, waiting for transfers between devices: 137 us -> none  [prefix_total(): overall = lax.psum(slab_values, 'depth')]
    all_gather x2 -> x0, waiting for transfers between devices: 75.6 us -> none  [entering(): pieces = lax.all_gather(value, axis)]
    pallas_call x0 -> x3, Pallas kernels: none -> 34.9 us  [the longest x1 21.8 us: on_device(): pl.pallas_call(functools.partial(slab_kernel, views, wide), out_shape=(ja...]
    all_to_all x0 -> x2, blocking collectives: none -> 31.3 us  [the longest x1 17.4 us: on_device(): up = lax.all_to_all(regroup(up, devices, part), ('depth', 'rows'), 0, 0)]
    dot_general x2 -> x0, matrix products: 14 us -> none  [strict_cumsum(): jnp.einsum('ij,vrjc->vric', strictly_lower, field, precision=lax.Precisio...]
    ppermute x4 -> x0, starting transfers between devices: 13.8 us -> none  [the longest x2 7.42 us: with_halo(): lax.ppermute(lax.slice_in_dim(block, block.shape[dim] - width, None, axis...]
    dynamic_slice x14 -> x0, local copies, waits for them, and re-layouts: 12.8 us -> none  [step(): longer = join(subtotal, pieces[position])]
    slice x4 -> x0, local copies, waits for them, and re-layouts: 8.53 us -> none  [the longest x2 4.92 us: shifted_pair(): from_right = jnp.pad(field[..., 1:], widths + [(0, 1)])]
  transfers between devices with their start and end apart: 8 -> 0, of which waited for: 6 -> 0; matrix products, arithmetic and copies ran while one was open for 7% -> 0% of each run, Pallas kernels for 0% -> 0%
where the time goes in v1:
time: 69.3 us; the launch traced here: 68.5 us
  Pallas kernels  34.9 us (50%)
  blocking collectives  31.3 us (45%)
  local copies, waits for them, and re-layouts  1.65 us (2%)
    pallas_call x1, Pallas kernels, on_device(): pl.pallas_call(functools.partial(slab_kernel, views, wide), out_shape=(ja...  21.8 us
    all_to_all x1, blocking collectives, on_device(): up = lax.all_to_all(regroup(up, devices, part), ('depth', 'rows'), 0, 0)  17.4 us
    all_to_all x1, blocking collectives, on_device(): lax.all_to_all(down, ('depth', 'rows'), 0, 0)  13.9 us
    pallas_call x1, Pallas kernels, on_device(): pl.pallas_call(functools.partial(gradient_kernel, views, wide), out_shape...  10.9 us
    pallas_call x1, Pallas kernels, on_device(): pl.pallas_call(functools.partial(column_kernel, views, slabs, rows), out_...  2.13 us
    unnamed x1, local copies, waits for them, and re-layouts  1.65 us

profile of v1, /device:TPU:1, one launch (start us, length us, event | category | flops | bytes accessed | tf_op | source)
XLA Modules:
  0.0 68.5 jit_solution(2809694095014225684)
XLA Ops:
  0.6 1.6 %copy.9 = f32[4,1,8192]{2,0,1:T(4,128)} copy(f32[4,1,8192]{2,1,0:T(1,128)} %param.7) | data formatting | bytes 262144
  2.3 21.8 %slab.1 = (f32[32,8,256]{2,1,0:T(8,128)}, f32[4,32,8192]{2,1,0:T(8,128)}, f32[4,32,8192]{2,1,0:T(8,128)}) custom-call(s32[4]{0:T(128)} %angle_ref.5, s32[4]{0:T(128)} %side_ref.3, s32[1]{0:T(128)} %bitcast.place_ref, f32[32,8192]{1,0:T(8,128)} %bitcast.8, f32[32,8192]{1,0:T(8,128)} %bitcast.9, f32[4,8192]{1,0:T(4,128)} %bitcast.10), custom_call_target="tpu_custom_call" | custom-call | tf_op jit(solution)/shard_map/slab/pallas_call | solution.py:225
  24.1 17.4 %all_to_all.10.up_ref = f32[32,8,256]{2,1,0:T(8,128)} all-to-all(f32[32,8,256]{2,1,0:T(8,128)} %get-tuple-element.7), channel_id=1, replica_groups=mesh['depth'=8,'rows'=4] {'depth','rows'}, dimensions={0} | all-to-all | bytes 524288 | tf_op jit(solution)/shard_map/all_to_all | solution.py:248
  41.6 2.1 %column.1 = f32[32,8,256]{2,1,0:T(8,128)} custom-call(s32[4]{0:T(128)} %angle_ref.5, s32[4]{0:T(128)} %side_ref.3, f32[32,8,256]{2,1,0:T(8,128)} %all_to_all.10.up_ref), custom_call_target="tpu_custom_call" | custom-call | tf_op jit(solution)/shard_map/column/pallas_call | solution.py:249
  43.7 13.9 %all_to_all.11.down_ref = f32[32,8,256]{2,1,0:T(8,128)} all-to-all(f32[32,8,256]{2,1,0:T(8,128)} %column.1), channel_id=1, replica_groups=mesh['depth'=8,'rows'=4] {'depth','rows'}, dimensions={0} | all-to-all | bytes 524288 | tf_op jit(solution)/shard_map/all_to_all | solution.py:256
  57.5 10.9 %gradient.1 = (f32[32,8192]{1,0:T(8,128)}, f32[32,8192]{1,0:T(8,128)}) custom-call(s32[4]{0:T(128)} %angle_ref.5, f32[32,8,256]{2,1,0:T(8,128)} %all_to_all.11.down_ref, f32[4,32,8192]{2,1,0:T(8,128)} %get-tuple-element.8.lt_ref, f32[4,32,8192]{2,1,0:T(8,128)} %get-tuple-element.9.lb_ref), custom_call_target="tpu_custom_call" | custom-call | tf_op jit(solution)/shard_map/gradient/pallas_call | solution.py:257

commit v2 on v0

v2 whole, which is shorter than its diff:
```python
import functools
import math

import jax
import jax.numpy as jnp
from jax import lax
from jax.experimental import pallas as pl
from jax.experimental.pallas import tpu as pltpu
from jax.sharding import PartitionSpec as P

ANGLES = 360
LANES, SUBS = 128, 8
GROUP = SUBS * SUBS
F32 = jnp.float32


def tilt_parts(angle):
    tilt = 0.8 * jnp.sin(jnp.pi * (angle.astype(F32) + 0.5) / ANGLES - jnp.pi / 2)
    return 1.0 - jnp.abs(tilt), jnp.maximum(tilt, 0.0), jnp.maximum(-tilt, 0.0)


def leans_right(angle):
    return 2 * angle >= ANGLES


def view_column(ref, views, shape):
    rows = lax.broadcasted_iota(jnp.int32, shape, 0)
    out = jnp.full(shape, ref[0], jnp.int32)
    for v in range(1, views):
        out = jnp.where(rows == v, ref[v], out)
    return out


def shift_tools():
    lane = lax.broadcasted_iota(jnp.int32, (SUBS, LANES), 1)

    def before(rolled, rolled_previous):
        return jnp.where(lane == 0, rolled_previous, rolled)

    def after(rolled, rolled_next):
        return jnp.where(lane == LANES - 1, rolled_next, rolled)

    return before, after, lambda x: pltpu.roll(x, 1, 1), lambda x: pltpu.roll(x, LANES - 1, 1)


def slab_kernel(
    views, angle_hbm, side_hbm, d_hbm, a_hbm, m_hbm, up_ref, lt_ref, front_ref,
    angle_ref, side_ref, raw_ref, ax_ref, dx_ref, m_ref, sem, sem_raw,
):
    blocks, length = raw_ref.shape[1:3]
    groups = length // GROUP
    place = lax.rem(lax.axis_index("depth"), views)
    small = [
        pltpu.make_async_copy(angle_hbm, angle_ref, sem.at[0]),
        pltpu.make_async_copy(side_hbm, side_ref, sem.at[1]),
        pltpu.make_async_copy(m_hbm.at[place], m_ref, sem.at[2]),
    ]

    def fetch(g):
        part = pl.ds(pl.multiple_of(g * GROUP, GROUP), GROUP)
        return [
            pltpu.make_async_copy(hbm.at[:, part], raw_ref.at[f, :, part], sem_raw.at[f, g])
            for f, hbm in enumerate((a_hbm, d_hbm))
        ]

    for g in range(groups):
        for copy in fetch(g):
            copy.start()
    for copy in small:
        copy.start()
    before, after, roll_up, roll_down = shift_tools()
    scale = -math.log2(math.e)

    for copy in fetch(0):
        copy.wait()
    for copy in small:
        copy.wait()

    def shifts(g, carry):
        base = pl.multiple_of(g * GROUP, GROUP)
        ahead = jnp.minimum(g + 1, groups - 1)

        @pl.when(g + 1 < groups)
        def _():
            for copy in fetch(ahead):
                copy.wait()

        first, last = g == 0, g + 1 == groups
        starts = [pl.multiple_of(jnp.maximum(base - SUBS, 0), SUBS)]
        starts += [pl.multiple_of(base + SUBS * i, SUBS) for i in range(SUBS)]
        starts += [pl.multiple_of(jnp.minimum(base + GROUP, length - SUBS), SUBS)]
        totals = [None] * (SUBS + 2)
        for f in range(2):
            for b in range(blocks):
                tiles = [raw_ref[f, b, pl.ds(at, SUBS), :] for at in starts]
                if f == 0:
                    tiles = [scale * x for x in tiles]
                tiles[0] = jnp.where(first, 0.0, tiles[0])
                tiles[-1] = jnp.where(last, 0.0, tiles[-1])
                up = [roll_up(x) for x in tiles[:-1]]
                down = [roll_down(x) for x in tiles[1:]]
                for i in range(SUBS):
                    at = pl.ds(starts[i + 1], SUBS)
                    here = tiles[i + 1]
                    left = before(up[i + 1], up[i]) - here
                    right = after(down[i], down[i + 1]) - here
                    if f == 0:
                        ax_ref[0, b, at, :] = here
                        ax_ref[1, b, at, :] = left
                        ax_ref[2, b, at, :] = right
                    else:
                        dx_ref[0, b, at, :] = left
                        dx_ref[1, b, at, :] = right
                if f == 0:
                    totals = [x if y is None else x + y for x, y in zip(tiles, totals)]
        totals = [jnp.sum(x, axis=0, keepdims=True) + jnp.zeros((SUBS, LANES), F32) for x in totals]
        up = [roll_up(x) for x in totals[:-1]]
        down = [roll_down(x) for x in totals[1:]]
        for i in range(SUBS):
            left = before(up[i + 1], up[i])
            right = after(down[i], down[i + 1])
            for row, value in enumerate((left, totals[i + 1], right)):
                up_ref[pl.ds(starts[i + 1] + views + row, 1), :] = value[:1]
        return carry

    lax.fori_loop(0, groups, shifts, 0)

    weights = []
    for v in range(views):
        _, left, right = tilt_parts(jnp.full((SUBS, LANES), angle_ref[v], jnp.int32))
        weights.append(left + right)
    shift = [jnp.where(leans_right(angle_ref[v]), 0, 1) for v in range(views)]
    far = [side_ref[v] == 1 for v in range(views)]

    def rays(g, carry):
        base = pl.multiple_of(g * GROUP, GROUP)
        depth = [jnp.zeros((SUBS, LANES), F32)] * views
        front = [jnp.zeros((SUBS, LANES), F32)] * views
        for i in range(blocks * SUBS):
            for v in range(views):
                b = jnp.where(far[v], blocks - 1 - i // SUBS, i // SUBS)
                at = pl.ds(base + jnp.where(far[v], SUBS - 1 - i % SUBS, i % SUBS), SUBS, stride=SUBS)
                light = jnp.exp2(depth[v])
                depth[v] = depth[v] + (ax_ref[0, b, at, :] + weights[v] * ax_ref[1 + shift[v], b, at, :])
                emission = raw_ref[1, b, at, :] + weights[v] * dx_ref[shift[v], b, at, :]
                front[v] = front[v] + emission * light
                lt_ref[v, b, at, :] = light
                front_ref[v, b, at, :] = front[v]
        for v in range(views):
            up_ref[pl.ds(base + v, SUBS, stride=SUBS), :] = front[v]
        up_ref[pl.ds(base + views + 3, SUBS, stride=SUBS), :] = m_ref[pl.ds(pl.multiple_of(g * SUBS, SUBS), SUBS), :]
        return carry

    lax.fori_loop(0, groups, rays, 0)


def column_kernel(views, slabs, rows, angle_ref, side_ref, up_ref, down_ref):
    height, wide = up_ref.shape[1:]
    shape = (views, wide)
    centre, left, right = tilt_parts(view_column(angle_ref, views, shape))
    far = view_column(side_ref, views, shape) == 1

    def blur(values):
        out = []
        for r in range(rows):
            total = 0.5 * values[r]
            if r > 0:
                total = total + 0.25 * values[r - 1]
            if r + 1 < rows:
                total = total + 0.25 * values[r + 1]
            out.append(total)
        return out

    for half in range(0, height, SUBS):
        passes, behinds, signals = {}, {}, []
        for r in range(rows):
            absorbs, runs = [], []
            run = jnp.zeros(shape, F32)
            for k in range(slabs):
                block = up_ref[k * rows + r, half : half + SUBS]
                absorb = left * block[views : views + 1] + centre * block[views + 1 : views + 2] + right * block[views + 2 : views + 3]
                runs.append(run)
                absorbs.append(absorb)
                run = run + absorb
            ends, starts = [], []
            signal = jnp.zeros(shape, F32)
            for k in range(slabs):
                entering = jnp.where(far, run - runs[k] - absorbs[k], runs[k])
                passes[k, r] = jnp.exp2(entering)
                starts.append(signal)
                signal = signal + passes[k, r] * up_ref[k * rows + r, half : half + views]
                ends.append(signal)
            for k in range(slabs):
                behinds[k, r] = jnp.where(far, -ends[k], starts[k] - signal)
            signals.append(signal)
        residuals = []
        for r, value in enumerate(blur(signals)):
            seen = [up_ref[v * rows + r, half + views + 3 : half + views + 4] for v in range(views)]
            residuals.append(value - jnp.concatenate(seen, axis=0))
        for r, back in enumerate(blur(residuals)):
            for k in range(slabs):
                scaled = back * behinds[k, r]
                parts = [back * passes[k, r]]
                for weight in (centre, left, right):
                    parts.append(jnp.sum(weight * scaled, axis=0, keepdims=True))
                parts.append(jnp.zeros((1, wide), F32))
                down_ref[k * rows + r, half : half + SUBS] = jnp.concatenate(parts, axis=0)


def gradient_kernel(views, angle_hbm, down_ref, lt_ref, front_ref, gd_hbm, ga_hbm, angle_ref, p_ref, out_ref, sem, sem_out):
    blocks, length = out_ref.shape[1:3]
    groups = length // GROUP
    copy = pltpu.make_async_copy(angle_hbm, angle_ref, sem)
    copy.start()
    copy.wait()
    before, after, roll_up, roll_down = shift_tools()
    right_of = [leans_right(angle_ref[v]).astype(jnp.int32) for v in range(views)]
    count = sum(right_of)
    order = [0] * views
    seen = [jnp.int32(0), jnp.int32(0)]
    for v in range(views):
        place = jnp.where(right_of[v] == 1, seen[0], count + seen[1])
        seen = [seen[0] + right_of[v], seen[1] + 1 - right_of[v]]
        order = [jnp.where(place == p, v, order[p]) for p in range(views)]
    weights = []
    for p in range(views):
        centre, left, right = tilt_parts(jnp.full((SUBS, LANES), angle_ref[order[p]], jnp.int32))
        weights.append((centre, left + right))

    def send(g):
        part = pl.ds(pl.multiple_of(g * GROUP, GROUP), GROUP)
        return [
            pltpu.make_async_copy(out_ref.at[q, :, part], hbm.at[:, part], sem_out.at[q, g])
            for q, hbm in enumerate((gd_hbm, ga_hbm))
        ]

    def products(ahead):
        def body(t, carry):
            at = pl.multiple_of(t * SUBS, SUBS)
            row = lambda f: jnp.broadcast_to(down_ref[pl.ds(at + f, 1), :], (SUBS, LANES))
            scales = []
            for p in range(views):
                back = row(order[p])
                scales.append((weights[p][0] * back, weights[p][1] * back))
            extra = [row(views + i) for i in range(3)]
            here = pl.ds(at, SUBS)
            for b in range(blocks):
                density, absorb = [None] * 3, list(extra)
                for p in range(views):
                    light = lt_ref[order[p], b, here, :]
                    front = front_ref[order[p], b, here, :]
                    for i, scale in ((0, scales[p][0]), (1 if p < ahead else 2, scales[p][1])):
                        density[i] = scale * light if density[i] is None else density[i] + scale * light
                        absorb[i] = absorb[i] + scale * front
                for i in range(3):
                    p_ref[0, i, b, here, :] = jnp.zeros((SUBS, LANES), F32) if density[i] is None else density[i]
                    p_ref[1, i, b, here, :] = absorb[i]
            return carry

        lax.fori_loop(0, groups * SUBS, body, 0)

    for ahead in range(views + 1):
        @pl.when(count == ahead)
        def _():
            products(ahead)

    def shifts(g, carry):
        base = pl.multiple_of(g * GROUP, GROUP)
        first, last = g == 0, g + 1 == groups
        own = [pl.multiple_of(base + SUBS * i, SUBS) for i in range(SUBS)]
        previous = pl.multiple_of(jnp.maximum(base - SUBS, 0), SUBS)
        following = pl.multiple_of(jnp.minimum(base + GROUP, length - SUBS), SUBS)
        for q in range(2):
            for b in range(blocks):
                up = [p_ref[q, 2, b, pl.ds(at, SUBS), :] for at in [previous] + own]
                down = [p_ref[q, 1, b, pl.ds(at, SUBS), :] for at in own + [following]]
                up[0] = jnp.where(first, 0.0, up[0])
                down[-1] = jnp.where(last, 0.0, down[-1])
                up = [roll_up(x) for x in up]
                down = [roll_down(x) for x in down]
                for i in range(SUBS):
                    at = pl.ds(own[i], SUBS)
                    value = p_ref[q, 0, b, at, :] + before(up[i + 1], up[i]) + after(down[i], down[i + 1])
                    out_ref[q, b, at, :] = value
        for copy in send(g):
            copy.start()
        return carry

    lax.fori_loop(0, groups, shifts, 0)
    for g in range(groups):
        for copy in send(g):
            copy.wait()


def on_device(density, attenuation, measured, angle_ids, sides):
    cells, columns = density.shape[1:]
    views = measured.shape[0]
    slabs, rows = lax.axis_size("depth"), lax.axis_size("rows")
    devices = slabs * rows
    assert views + 4 == SUBS and slabs >= views and cells % SUBS == 0 and columns % (SUBS * LANES) == 0
    part = columns // devices
    blocks, tiles = cells // SUBS, columns // LANES
    length = tiles * SUBS
    smem = pl.BlockSpec(memory_space=pltpu.SMEM)
    vmem = pl.BlockSpec(memory_space=pltpu.VMEM)
    leave = pl.BlockSpec(memory_space=pl.ANY)

    def in_hbm(x):
        return pltpu.with_memory_space_constraint(x, pltpu.HBM)

    def tiled(x):
        return x.reshape(blocks, SUBS, tiles, LANES).transpose(0, 2, 1, 3).reshape(blocks, length, LANES)

    def untiled(x):
        return x.reshape(blocks, tiles, SUBS, LANES).transpose(0, 2, 1, 3).reshape(1, cells, columns)

    field = pltpu.VMEM((views, blocks, length, LANES), F32)
    up, light, front = pl.pallas_call(
        functools.partial(slab_kernel, views),
        out_shape=(pltpu.VMEM((length, LANES), F32), field, field),
        in_specs=[leave] * 5,
        out_specs=(vmem,) * 3,
        scratch_shapes=[
            pltpu.SMEM((views,), jnp.int32),
            pltpu.SMEM((views,), jnp.int32),
            pltpu.VMEM((2, blocks, length, LANES), F32),
            pltpu.VMEM((3, blocks, length, LANES), F32),
            pltpu.VMEM((2, blocks, length, LANES), F32),
            pltpu.VMEM((tiles, LANES), F32),
            pltpu.SemaphoreType.DMA((3,)),
            pltpu.SemaphoreType.DMA((2, tiles // SUBS)),
        ],
        compiler_params=pltpu.CompilerParams(vmem_limit_bytes=32 << 20),
        name="slab",
    )(in_hbm(angle_ids), in_hbm(sides), in_hbm(tiled(density[0])), in_hbm(tiled(attenuation[0])), in_hbm(measured.reshape(views, tiles, LANES)))

    def to_parts(x):
        if part % LANES == 0:
            return x.reshape(devices, part // LANES * SUBS, LANES)
        x = x.reshape(tiles, SUBS, LANES).transpose(1, 0, 2).reshape(SUBS, devices, part)
        return x.transpose(1, 0, 2)

    def from_parts(x):
        if part % LANES == 0:
            return x.reshape(length, LANES)
        x = x.transpose(1, 0, 2).reshape(SUBS, tiles, LANES)
        return x.transpose(1, 0, 2).reshape(length, LANES)

    up = lax.all_to_all(to_parts(up), ("depth", "rows"), 0, 0)
    down = pl.pallas_call(
        functools.partial(column_kernel, views, slabs, rows),
        out_shape=jax.ShapeDtypeStruct(up.shape, F32),
        in_specs=[smem] * 2 + [vmem],
        out_specs=vmem,
        compiler_params=pltpu.CompilerParams(vmem_limit_bytes=16 << 20),
        name="column",
    )(angle_ids, sides, up)
    down = from_parts(lax.all_to_all(down, ("depth", "rows"), 0, 0))
    grads = pl.pallas_call(
        functools.partial(gradient_kernel, views),
        out_shape=(pltpu.HBM((blocks, length, LANES), F32),) * 2,
        in_specs=[leave] + [vmem] * 3,
        out_specs=(leave,) * 2,
        scratch_shapes=[
            pltpu.SMEM((views,), jnp.int32),
            pltpu.VMEM((2, 3, blocks, length, LANES), F32),
            pltpu.VMEM((2, blocks, length, LANES), F32),
            pltpu.SemaphoreType.DMA,
            pltpu.SemaphoreType.DMA((2, tiles // SUBS)),
        ],
        compiler_params=pltpu.CompilerParams(vmem_limit_bytes=32 << 20),
        name="gradient",
    )(in_hbm(angle_ids), down, light, front)
    return untiled(grads[0]), untiled(grads[1])


def solution(mesh):
    placed = (P("rows", "depth", None), P("rows", "depth", None), P(None, "rows", None), P(), P())
    return jax.shard_map(
        on_device,
        mesh=mesh,
        in_specs=placed,
        out_specs=(P("rows", "depth", None), P("rows", "depth", None)),
        check_vma=False,
    )
```

time: 302 us -> 48.1 us (0.16)
  waiting for transfers between devices: 216 us -> 0 us
  blocking collectives: 0 us -> 29.9 us
  local copies, waits for them, and re-layouts: 27.4 us -> 1.31 us
  Pallas kernels: 0 us -> 15.5 us
  other arithmetic: 15.5 us -> 0 us
  matrix products: 14 us -> 0 us
  starting transfers between devices: 13.9 us -> 0 us
  between operations: 14 us -> 0.65 us
    psum x2 -> x0, waiting for transfers between devices: 137 us -> none  [prefix_total(): overall = lax.psum(slab_values, 'depth')]
    all_gather x2 -> x0, waiting for transfers between devices: 75.6 us -> none  [entering(): pieces = lax.all_gather(value, axis)]
    all_to_all x0 -> x2, blocking collectives: none -> 29.9 us  [the longest x1 17.1 us: on_device(): up = lax.all_to_all(to_parts(up), ('depth', 'rows'), 0, 0)]
    pallas_call x0 -> x3, Pallas kernels: none -> 15.5 us  [the longest x1 9.2 us: on_device(): pl.pallas_call(functools.partial(slab_kernel, views), out_shape=(pltpu.VM...]
    dot_general x2 -> x0, matrix products: 14 us -> none  [strict_cumsum(): jnp.einsum('ij,vrjc->vric', strictly_lower, field, precision=lax.Precisio...]
    ppermute x4 -> x0, starting transfers between devices: 13.8 us -> none  [the longest x2 7.42 us: with_halo(): lax.ppermute(lax.slice_in_dim(block, block.shape[dim] - width, None, axis...]
    dynamic_slice x14 -> x0, local copies, waits for them, and re-layouts: 12.8 us -> none  [step(): longer = join(subtotal, pieces[position])]
    slice x4 -> x0, local copies, waits for them, and re-layouts: 8.53 us -> none  [the longest x2 4.92 us: shifted_pair(): from_right = jnp.pad(field[..., 1:], widths + [(0, 1)])]
  transfers between devices with their start and end apart: 8 -> 0, of which waited for: 6 -> 0; matrix products, arithmetic and copies ran while one was open for 7% -> 0% of each run, Pallas kernels for 0% -> 0%
where the time goes in v2:
time: 48.1 us; the launch traced here: 47.3 us
  blocking collectives  29.9 us (62%)
  Pallas kernels  15.5 us (32%)
  local copies, waits for them, and re-layouts  1.31 us (3%)
  between operations  0.65 us (1%)
    all_to_all x1, blocking collectives, on_device(): up = lax.all_to_all(to_parts(up), ('depth', 'rows'), 0, 0)  17.1 us
    all_to_all x1, blocking collectives, on_device(): down = from_parts(lax.all_to_all(down, ('depth', 'rows'), 0, 0))  12.8 us
    pallas_call x1, Pallas kernels, on_device(): pl.pallas_call(functools.partial(slab_kernel, views), out_shape=(pltpu.VM...  9.2 us
    pallas_call x1, Pallas kernels, on_device(): pl.pallas_call(functools.partial(gradient_kernel, views), out_shape=(pltp...  5.28 us
    unnamed x4, local copies, waits for them, and re-layouts  1.31 us
    pallas_call x1, Pallas kernels, on_device(): pl.pallas_call(functools.partial(column_kernel, views, slabs, rows), out_...  0.99 us

profile of v2, /device:TPU:1, one launch (start us, length us, event | category | flops | bytes accessed | tf_op | source)
XLA Modules:
  0.0 47.3 jit_solution(11357895911743062717)
XLA Ops:
  0.6 9.2 %slab.1 = (f32[512,128]{1,0:T(8,128)S(1)}, f32[4,4,512,128]{3,2,1,0:T(8,128)S(1)}, f32[4,4,512,128]{3,2,1,0:T(8,128)S(1)}) custom-call(s32[4]{0:T(128)} %angle_hbm.3, s32[4]{0:T(128)} %side_ref.1, f32[4,512,128]{2,1,0:T(8,128)} %bitcast.25, f32[4,512,128]{2,1,0:T(8,128)} %bitcast.26, f32[4,64,128]{2,1,0:T(8,128)} %bitcast.27), custom_call_target="tpu_custom_call" | custom-call | tf_op jit(solution)/shard_map/slab/pallas_call | solution.py:318
  9.8 17.1 %all_to_all.10.up_ref = f32[32,16,128]{2,1,0:T(8,128)S(1)} all-to-all(f32[32,16,128]{2,1,0:T(8,128)S(1)} %bitcast.24), channel_id=1, replica_groups=mesh['depth'=8,'rows'=4] {'depth','rows'}, dimensions={0} | all-to-all | bytes 524288 | tf_op jit(solution)/shard_map/all_to_all | solution.py:349
  27.0 0.0 copy-start
  27.0 0.7 %copy-done = s32[4]{0:T(128)S(1)} copy-done((s32[4]{0:T(128)S(1)}, s32[4]{0:T(128)}, u32[]{:S(2)}) %copy-start) | copy-done | bytes 40
  27.6 0.0 copy-start.1
  27.6 0.7 %copy-done.1 = s32[4]{0:T(128)S(1)} copy-done((s32[4]{0:T(128)S(1)}, s32[4]{0:T(128)}, u32[]{:S(2)}) %copy-start.1) | copy-done | bytes 40
  28.3 1.0 %column.1 = f32[32,16,128]{2,1,0:T(8,128)S(1)} custom-call(s32[4]{0:T(128)S(1)} %copy-done, s32[4]{0:T(128)S(1)} %copy-done.1, f32[32,16,128]{2,1,0:T(8,128)S(1)} %all_to_all.10.up_ref), custom_call_target="tpu_custom_call" | custom-call | tf_op jit(solution)/shard_map/column/pallas_call | solution.py:350
  29.3 12.8 %all_to_all.11 = f32[32,16,128]{2,1,0:T(8,128)S(1)} all-to-all(f32[32,16,128]{2,1,0:T(8,128)S(1)} %column.1), channel_id=1, replica_groups=mesh['depth'=8,'rows'=4] {'depth','rows'}, dimensions={0} | all-to-all | bytes 524288 | tf_op jit(solution)/shard_map/all_to_all | solution.py:358
  42.0 5.3 %gradient.1 = (f32[4,512,128]{2,1,0:T(8,128)}, f32[4,512,128]{2,1,0:T(8,128)}) custom-call(s32[4]{0:T(128)} %angle_hbm.3, f32[512,128]{1,0:T(8,128)S(1)} %bitcast.23, f32[4,4,512,128]{3,2,1,0:T(8,128)S(1)} %get-tuple-element.8.lt_ref, f32[4,4,512,128]{3,2,1,0:T(8,128)S(1)} %get-tuple-element.9.front_ref), custom_call_target="tpu_custom_call" | custom-call | tf_op jit(solution)/shard_map/gradient/pallas_call | solution.py:359
Async XLA Ops:
  27.0 0.7 %copy-start = (s32[4]{0:T(128)S(1)}, s32[4]{0:T(128)}, u32[]{:S(2)}) copy-start(s32[4]{0:T(128)} %angle_hbm.3) | copy-start | bytes 52
  27.6 0.7 %copy-start.1 = (s32[4]{0:T(128)S(1)}, s32[4]{0:T(128)}, u32[]{:S(2)}) copy-start(s32[4]{0:T(128)} %side_ref.1) | copy-start | bytes 52

commit v3 on v0

v3 whole, which is shorter than its diff:
```python
import functools
import math

import jax
import jax.numpy as jnp
from jax import lax
from jax.experimental import pallas as pl
from jax.experimental.pallas import tpu as pltpu
from jax.sharding import PartitionSpec as P

ANGLES = 360
LANES, SUBS = 128, 8
GROUP = SUBS * SUBS
TILE = (SUBS, LANES)
F32 = jnp.float32


def tilt_parts(angle):
    tilt = 0.8 * jnp.sin(jnp.pi * (angle.astype(F32) + 0.5) / ANGLES - jnp.pi / 2)
    return 1.0 - jnp.abs(tilt), jnp.maximum(tilt, 0.0), jnp.maximum(-tilt, 0.0)


def leans_right(angle):
    return 2 * angle >= ANGLES


def near_first(sides, views):
    order = [0] * views
    seen = [jnp.int32(0), jnp.int32(views // 2)]
    for v in range(views):
        far = (sides[v] == 1).astype(jnp.int32)
        place = jnp.where(far == 1, seen[1], seen[0])
        seen = [seen[0] + 1 - far, seen[1] + far]
        order = [jnp.where(place == p, v, order[p]) for p in range(views)]
    return order


def lanes():
    return lax.broadcasted_iota(jnp.int32, TILE, 1)


def subs():
    return lax.broadcasted_iota(jnp.int32, TILE, 0)


def spread(row):
    return jnp.broadcast_to(row, TILE)


def moved_right(blocks):
    first_lane, first_sub = lanes() == 0, subs() == 0
    out, carried = [], jnp.zeros(TILE, F32)
    for x in blocks:
        rolled = pltpu.roll(x, 1, 1)
        down = pltpu.roll(rolled, 1, 0)
        out.append(jnp.where(first_lane, jnp.where(first_sub, carried, down), rolled))
        carried = down
    return out


def moved_left(blocks):
    last_lane, last_sub = lanes() == LANES - 1, subs() == SUBS - 1
    out, carried = [], jnp.zeros(TILE, F32)
    for x in reversed(blocks):
        rolled = pltpu.roll(x, LANES - 1, 1)
        up = pltpu.roll(rolled, SUBS - 1, 0)
        out.append(jnp.where(last_lane, jnp.where(last_sub, carried, up), rolled))
        carried = up
    return out[::-1]


def slab_kernel(
    views, slabs, angle_hbm, side_hbm, d_hbm, a_hbm, m_hbm, up_ref, tilt_ref, field_ref,
    angle_ref, side_ref, raw_ref, ax_ref, dx_ref, sum_ref, m_ref, sem, sem_raw,
):
    blocks, length = raw_ref.shape[1:3]
    cells, groups, fields = blocks * SUBS, length // GROUP, views + 2
    slab = lax.axis_index("depth")
    share = max(slabs // views, 1)

    def fetch(b):
        return [pltpu.make_async_copy(hbm.at[b], raw_ref.at[f, b], sem_raw.at[f, b]) for f, hbm in enumerate((a_hbm, d_hbm))]

    small = [pltpu.make_async_copy(angle_hbm, angle_ref, sem.at[0]), pltpu.make_async_copy(side_hbm, side_ref, sem.at[1])]
    for copy in small + [copy for b in range(blocks) for copy in fetch(b)]:
        copy.start()
    for copy in small:
        copy.wait()
    order = near_first(side_ref, views)
    seen = jnp.int32(0)
    for p in range(views):
        seen = jnp.where(lax.rem(slab // share, views) == p, order[p], seen)
    fetch_m = pltpu.make_async_copy(m_hbm.at[seen], m_ref, sem.at[2])
    fetch_m.start()
    angle_block = jnp.zeros(TILE, jnp.int32)
    for p in range(views):
        angle_block = jnp.where(subs() == p, angle_ref[order[p]], angle_block)
    parts = tilt_parts(angle_block)
    for i, part in enumerate(parts):
        tilt_ref[i] = part
    beside = parts[1] + parts[2]
    weights = [spread(beside[p : p + 1]) for p in range(views)]
    shift = [jnp.where(leans_right(angle_ref[order[p]]), 0, 1) for p in range(views)]
    scale = -math.log2(math.e)
    sum_ref[...] = jnp.zeros(sum_ref.shape, F32)

    def shifts(z, carry):
        b = z // SUBS
        row = lax.rem(z, SUBS)

        @pl.when(row == 0)
        def _():
            for copy in fetch(b):
                copy.wait()

        absorbs = [scale * raw_ref[0, b, pl.ds(g * GROUP + row, SUBS, stride=SUBS), :] for g in range(groups)]
        for g, (here, left, right) in enumerate(zip(absorbs, moved_right(absorbs), moved_left(absorbs))):
            ax_ref[0, z, g] = here
            ax_ref[1, z, g] = left - here
            ax_ref[2, z, g] = right - here
            sum_ref[g] = sum_ref[g] + here
        density = [raw_ref[1, b, pl.ds(g * GROUP + row, SUBS, stride=SUBS), :] for g in range(groups)]
        for g, (here, left, right) in enumerate(zip(density, moved_right(density), moved_left(density))):
            dx_ref[0, z, g] = here
            dx_ref[1, z, g] = left - here
            dx_ref[2, z, g] = right - here
        return carry

    lax.fori_loop(0, cells, shifts, 0)

    def put(g, field, value):
        up_ref[pl.ds(g * SUBS * fields + field, SUBS, stride=fields), :] = value

    def rays(g, carry):
        depth = [jnp.zeros(TILE, F32)] * views
        front = [jnp.zeros(TILE, F32)] * views
        for i in range(cells):
            for p in range(views):
                z = i if p < views // 2 else cells - 1 - i
                light = jnp.exp2(depth[p])
                depth[p] = depth[p] + (ax_ref[0, z, g] + weights[p] * ax_ref[1 + shift[p], z, g])
                front[p] = front[p] + (dx_ref[0, z, g] + weights[p] * dx_ref[1 + shift[p], z, g]) * light
                field_ref[0, p, z, g] = light
                field_ref[1, p, z, g] = front[p]
        for p in range(views):
            put(g, p, front[p])
        return carry

    lax.fori_loop(0, groups, rays, 0)
    fetch_m.wait()
    totals = [sum_ref[g] for g in range(groups)]
    odd = lax.rem(subs(), 2) == 1
    second = lax.rem(slab, share) == 1
    for g, (before, after) in enumerate(zip(moved_right(totals), moved_left(totals))):
        counts = m_ref[pl.ds(g * SUBS, SUBS), :]
        counts = jnp.where(second, pltpu.roll(counts, SUBS - 1, 0), counts)
        edges = jnp.where(lanes() == 0, pltpu.roll(before, 1, 0), after)
        put(g, views, totals[g])
        put(g, views + 1, jnp.where(odd, edges, counts))


def blur(values):
    out = []
    for r in range(len(values)):
        total = 0.5 * values[r]
        if r > 0:
            total = total + 0.25 * values[r - 1]
        if r + 1 < len(values):
            total = total + 0.25 * values[r + 1]
        out.append(total)
    return out


def column_kernel(views, rows, tilt_ref, up_ref, down_ref):
    fields = views + 2
    record = 2 * fields
    first_lane, last_lane, sub = lanes() == 0, lanes() == LANES - 1, subs()
    weights = [[spread(tilt_ref[i, p : p + 1]) for i in range(3)] for p in range(views)]

    def get(r, half, field):
        return up_ref[pl.ds(r * record + half * fields + field, SUBS, stride=rows * record), :]

    def put(r, half, field, value):
        down_ref[pl.ds(r * record + half * fields + field, SUBS, stride=rows * record), :] = value

    def scan(value, far):
        step = 1
        while step < SUBS:
            if far:
                value = value + jnp.where(sub >= step, pltpu.roll(value, step, 0), 0.0)
            else:
                value = value + jnp.where(sub < SUBS - step, pltpu.roll(value, SUBS - step, 0), 0.0)
            step *= 2
        return value

    passes, behinds = {}, {}
    signals = {(p, half): [] for p in range(views) for half in range(2)}
    for r in range(rows):
        total = [get(r, half, views) for half in range(2)]
        edges = get(r, 1, views + 1)
        up = [pltpu.roll(x, 1, 1) for x in total]
        down = [pltpu.roll(x, LANES - 1, 1) for x in total]
        before = [jnp.where(first_lane, edges, up[0]), jnp.where(first_lane, up[0], up[1])]
        after = [jnp.where(last_lane, down[1], down[0]), jnp.where(last_lane, edges, down[1])]
        for half in range(2):
            for p in range(views):
                far = p >= views // 2
                centre, left, right = weights[p]
                absorb = centre * total[half] + left * before[half] + right * after[half]
                entering = scan(absorb, not far) - absorb
                light = jnp.exp2(entering)
                behind = scan(light * get(r, half, p), far)
                passes[r, half, p] = light
                behinds[r, half, p] = behind
                edge = SUBS - 1 if far else 0
                signals[p, half].append(spread(behind[edge : edge + 1]))
    backs = {}
    for p in range(views):
        for half in range(2):
            residuals = []
            for r, value in enumerate(blur(signals[p, half])):
                at = ((p * (SUBS // views) + half) * rows + r) * record + views + 1
                residuals.append(value - spread(up_ref[pl.ds(at, 1), :]))
            backs[p, half] = blur(residuals)
    for r in range(rows):
        sums = []
        for half in range(2):
            parts = [jnp.zeros(TILE, F32)] * 3
            for p in range(views):
                back = backs[p, half][r]
                put(r, half, p, back * passes[r, half, p])
                scaled = back * behinds[r, half, p]
                parts = [part - weight * scaled for part, weight in zip(parts, weights[p])]
            sums.append(parts)
        next_up = [pltpu.roll(sums[half][1], LANES - 1, 1) for half in range(2)]
        previous = [pltpu.roll(sums[half][2], 1, 1) for half in range(2)]
        zero = jnp.zeros(TILE, F32)
        put(r, 0, views, sums[0][0] + jnp.where(last_lane, next_up[1], next_up[0]) + jnp.where(first_lane, zero, previous[0]))
        put(r, 1, views, sums[1][0] + jnp.where(last_lane, zero, next_up[1]) + jnp.where(first_lane, previous[0], previous[1]))
        put(r, 0, views + 1, jnp.where(last_lane, next_up[0], zero))
        put(r, 1, views + 1, jnp.where(first_lane, previous[1], zero))


def wide_column_kernel(views, slabs, rows, tilt_ref, up_ref, down_ref):
    wide = up_ref.shape[2]
    shape = (views, wide)
    centre, left, right = [tilt_ref[i, :views, :1] for i in range(3)]
    far = lax.broadcasted_iota(jnp.int32, shape, 0) >= views // 2
    passes, behinds, signals = {}, {}, []
    for r in range(rows):
        absorbs, runs = [], []
        run = jnp.zeros(shape, F32)
        for k in range(slabs):
            block = up_ref[k * rows + r]
            absorb = left * block[views : views + 1] + centre * block[views + 1 : views + 2] + right * block[views + 2 : views + 3]
            runs.append(run)
            absorbs.append(absorb)
            run = run + absorb
        ends, starts = [], []
        signal = jnp.zeros(shape, F32)
        for k in range(slabs):
            entering = jnp.where(far, run - runs[k] - absorbs[k], runs[k])
            passes[k, r] = jnp.exp2(entering)
            starts.append(signal)
            signal = signal + passes[k, r] * up_ref[k * rows + r, :views]
            ends.append(signal)
        for k in range(slabs):
            behinds[k, r] = jnp.where(far, -ends[k], starts[k] - signal)
        signals.append(signal)
    residuals = []
    for r, value in enumerate(blur(signals)):
        seen = [up_ref[(v * max(slabs // views, 1)) * rows + r, views + 3 : views + 4] for v in range(views)]
        residuals.append(value - jnp.concatenate(seen, axis=0))
    for r, back in enumerate(blur(residuals)):
        for k in range(slabs):
            scaled = back * behinds[k, r]
            parts = [back * passes[k, r]]
            for weight in (centre, left, right):
                parts.append(jnp.sum(weight * scaled, axis=0, keepdims=True))
            parts.append(jnp.zeros((1, wide), F32))
            down_ref[k * rows + r] = jnp.concatenate(parts, axis=0)


def gradient_kernel(views, tilt_ref, down_ref, field_ref, gd_hbm, ga_hbm, scale_ref, out_ref, sem_out):
    cells, groups = field_ref.shape[2:4]
    fields = views + 2

    def send(b):
        return [pltpu.make_async_copy(out_ref.at[q, b], hbm.at[b], sem_out.at[q, b]) for q, hbm in enumerate((gd_hbm, ga_hbm))]

    def get(g, field):
        return down_ref[pl.ds(g * SUBS * fields + field, SUBS, stride=fields), :]

    for p in range(views):
        centre, left, right = [spread(tilt_ref[i, p : p + 1]) for i in range(3)]
        for g in range(groups):
            back = get(g, p)
            scale_ref[0, p, g] = centre * back
            scale_ref[1, p, g] = (left + right) * back
    odd = lax.rem(subs(), 2) == 1
    extras = [get(g, views + 1) for g in range(groups)]
    zero = jnp.zeros(TILE, F32)
    for g in range(groups):
        later = pltpu.roll(extras[g], SUBS - 1, 0)
        ahead = pltpu.roll(extras[g + 1], SUBS - 1, 0) if g + 1 < groups else zero
        later = jnp.where(subs() == SUBS - 1, ahead, later)
        earlier = pltpu.roll(extras[g], 1, 0)
        past = pltpu.roll(extras[g - 1], 1, 0) if g > 0 else zero
        earlier = jnp.where(subs() == 0, past, earlier)
        scale_ref[2, 0, g] = get(g, views) + jnp.where(odd, later, earlier)

    right_of = [(tilt_ref[1, p, 0] > 0.0).astype(jnp.int32) for p in range(views)]
    count = sum(right_of)
    order = [0] * views
    seen = [jnp.int32(0), count]
    for v in range(views):
        place = jnp.where(right_of[v] == 1, seen[0], seen[1])
        seen = [seen[0] + right_of[v], seen[1] + 1 - right_of[v]]
        order = [jnp.where(place == p, v, order[p]) for p in range(views)]

    def products(ahead):
        def body(z, carry):
            b, row = z // SUBS, lax.rem(z, SUBS)
            sums = [[], [], [], [], [], []]
            for g in range(groups):
                for q in range(2):
                    parts = [scale_ref[2, 0, g] if q == 1 else None, None, None]
                    for p in range(views):
                        value = field_ref[q, order[p], z, g]
                        for i, scale in ((0, scale_ref[0, order[p], g]), (1 if p < ahead else 2, scale_ref[1, order[p], g])):
                            parts[i] = scale * value if parts[i] is None else parts[i] + scale * value
                    for i in range(3):
                        sums[3 * q + i].append(parts[i])
            for q in range(2):
                total = sums[3 * q]
                if ahead > 0:
                    total = [x + y for x, y in zip(total, moved_left(sums[3 * q + 1]))]
                if ahead < views:
                    total = [x + y for x, y in zip(total, moved_right(sums[3 * q + 2]))]
                for g in range(groups):
                    out_ref[q, b, pl.ds(g * GROUP + row, SUBS, stride=SUBS), :] = total[g]

            @pl.when(row == SUBS - 1)
            def _():
                for copy in send(b):
                    copy.start()

            return carry

        lax.fori_loop(0, cells, body, 0)

    for ahead in range(views + 1):

        @pl.when(count == ahead)
        def _():
            products(ahead)

    for b in range(cells // SUBS):
        for copy in send(b):
            copy.wait()


def on_device(density, attenuation, measured, angle_ids, sides):
    cells, columns = density.shape[1:]
    views = measured.shape[0]
    slabs, rows = lax.axis_size("depth"), lax.axis_size("rows")
    devices = slabs * rows
    assert views == 4 and slabs % views == 0 and cells % SUBS == 0 and columns % (SUBS * LANES) == 0
    part = columns // devices
    compact = slabs == SUBS and part == 2 * LANES
    blocks, tiles = cells // SUBS, columns // LANES
    groups, length, fields = tiles // SUBS, tiles * SUBS, views + 2
    vmem = pl.BlockSpec(memory_space=pltpu.VMEM)
    leave = pl.BlockSpec(memory_space=pl.ANY)

    def grant(mib):
        return pltpu.CompilerParams(vmem_limit_bytes=mib << 20)

    def in_hbm(x):
        return pltpu.with_memory_space_constraint(x, pltpu.HBM)

    def tiled(x):
        return x.reshape(blocks, SUBS, tiles, LANES).transpose(0, 2, 1, 3).reshape(blocks, length, LANES)

    def untiled(x):
        return x.reshape(blocks, tiles, SUBS, LANES).transpose(0, 2, 1, 3).reshape(1, cells, columns)

    ids_in = [in_hbm(angle_ids), in_hbm(sides)]
    ids = [pltpu.SMEM((views,), jnp.int32)] * 2
    field = pltpu.VMEM((2, views, cells, groups) + TILE, F32)
    shifted = pltpu.VMEM((3, cells, groups, SUBS, LANES), F32)
    up, tilts, light = pl.pallas_call(
        functools.partial(slab_kernel, views, slabs),
        out_shape=(pltpu.VMEM((tiles * fields, LANES), F32), pltpu.VMEM((3,) + TILE, F32), field),
        in_specs=[leave] * 5,
        out_specs=(vmem,) * 3,
        scratch_shapes=ids
        + [
            pltpu.VMEM((2, blocks, length, LANES), F32),
            shifted,
            shifted,
            pltpu.VMEM((groups,) + TILE, F32),
            pltpu.VMEM((tiles, LANES), F32),
            pltpu.SemaphoreType.DMA((3,)),
            pltpu.SemaphoreType.DMA((2, blocks)),
        ],
        compiler_params=grant(24),
        name="slab",
    )(
        *ids_in,
        in_hbm(tiled(density[0])),
        in_hbm(tiled(attenuation[0])),
        in_hbm(measured.reshape(views, tiles, LANES)),
    )

    def exchange(x):
        return lax.all_to_all(x, ("depth", "rows"), 0, 0, tiled=True)

    if compact:
        rows_of = (devices * 2 * fields // 4, 4, LANES)
        up = exchange(up.reshape(rows_of)).reshape(tiles * fields, LANES)
    else:
        flat = up.reshape(tiles, fields, LANES).transpose(1, 0, 2).reshape(fields, columns)
        total = flat[views : views + 1]
        order = jnp.argsort(sides, stable=True)
        place = lax.rem(lax.axis_index("depth") // (slabs // views), views)
        counts = lax.dynamic_index_in_dim(measured[:, 0], order[place], 0)
        before = jnp.pad(total[:, :-1], ((0, 0), (1, 0)))
        after = jnp.pad(total[:, 1:], ((0, 0), (0, 1)))
        flat = jnp.concatenate([flat[:views], before, total, after, counts], axis=0)
        up = exchange(flat.reshape(SUBS, devices, part).transpose(1, 0, 2))
    kernel = functools.partial(column_kernel, views, rows) if compact else functools.partial(wide_column_kernel, views, slabs, rows)
    down = pl.pallas_call(
        kernel,
        out_shape=pltpu.VMEM(up.shape, F32) if compact else jax.ShapeDtypeStruct(up.shape, F32),
        in_specs=[vmem] * 2,
        out_specs=vmem,
        compiler_params=grant(4 if compact else 16),
        name="column",
    )(tilts, up)
    if compact:
        down = exchange(down.reshape(rows_of)).reshape(tiles * fields, LANES)
    else:
        flat = exchange(down).transpose(1, 0, 2).reshape(SUBS, columns)
        base = flat[views] + jnp.pad(flat[views + 1, 1:], (0, 1)) + jnp.pad(flat[views + 2, :-1], (1, 0))
        flat = jnp.concatenate([flat[:views], base[None], jnp.zeros((1, columns), F32)], axis=0)
        down = flat.reshape(fields, tiles, LANES).transpose(1, 0, 2).reshape(tiles * fields, LANES)
    grads = pl.pallas_call(
        functools.partial(gradient_kernel, views),
        out_shape=(pltpu.HBM((blocks, length, LANES), F32),) * 2,
        in_specs=[vmem] * 3,
        out_specs=(leave,) * 2,
        scratch_shapes=[
            pltpu.VMEM((3, views, groups) + TILE, F32),
            pltpu.VMEM((2, blocks, length, LANES), F32),
            pltpu.SemaphoreType.DMA((2, blocks)),
        ],
        compiler_params=grant(8),
        name="gradient",
    )(tilts, down, light)
    return untiled(grads[0]), untiled(grads[1])


def solution(mesh):
    placed = (P("rows", "depth", None), P("rows", "depth", None), P(None, "rows", None), P(), P())
    return jax.shard_map(
        on_device,
        mesh=mesh,
        in_specs=placed,
        out_specs=(P("rows", "depth", None), P("rows", "depth", None)),
        check_vma=False,
    )
```

time: 302 us -> 40 us (0.13)
  waiting for transfers between devices: 216 us -> 0 us
  blocking collectives: 0 us -> 27.5 us
  local copies, waits for them, and re-layouts: 27.4 us -> 0 us
  other arithmetic: 15.5 us -> 0 us
  matrix products: 14 us -> 0 us
  starting transfers between devices: 13.9 us -> 0 us
  between operations: 14 us -> 0.65 us
  Pallas kernels: 0 us -> 11.7 us
    psum x2 -> x0, waiting for transfers between devices: 137 us -> none  [prefix_total(): overall = lax.psum(slab_values, 'depth')]
    all_gather x2 -> x0, waiting for transfers between devices: 75.6 us -> none  [entering(): pieces = lax.all_gather(value, axis)]
    all_to_all x0 -> x2, blocking collectives: none -> 27.5 us  [exchange(): return lax.all_to_all(x, ('depth', 'rows'), 0, 0, tiled=True)]
    dot_general x2 -> x0, matrix products: 14 us -> none  [strict_cumsum(): jnp.einsum('ij,vrjc->vric', strictly_lower, field, precision=lax.Precisio...]
    ppermute x4 -> x0, starting transfers between devices: 13.8 us -> none  [the longest x2 7.42 us: with_halo(): lax.ppermute(lax.slice_in_dim(block, block.shape[dim] - width, None, axis...]
    dynamic_slice x14 -> x0, local copies, waits for them, and re-layouts: 12.8 us -> none  [step(): longer = join(subtotal, pieces[position])]
    pallas_call x0 -> x3, Pallas kernels: none -> 11.7 us  [the longest x1 6.44 us: on_device(): pl.pallas_call(functools.partial(slab_kernel, views, slabs), out_shape=(p...]
    slice x4 -> x0, local copies, waits for them, and re-layouts: 8.53 us -> none  [the longest x2 4.92 us: shifted_pair(): from_right = jnp.pad(field[..., 1:], widths + [(0, 1)])]
  transfers between devices with their start and end apart: 8 -> 0, of which waited for: 6 -> 0; matrix products, arithmetic and copies ran while one was open for 7% -> 0% of each run, Pallas kernels for 0% -> 0%
where the time goes in v3:
time: 40 us; the launch traced here: 39.9 us
  blocking collectives  27.5 us (69%)
  Pallas kernels  11.7 us (29%)
  between operations  0.65 us (2%)
    all_to_all x2, blocking collectives, exchange(): return lax.all_to_all(x, ('depth', 'rows'), 0, 0, tiled=True)  27.5 us
    pallas_call x1, Pallas kernels, on_device(): pl.pallas_call(functools.partial(slab_kernel, views, slabs), out_shape=(p...  6.44 us
    pallas_call x1, Pallas kernels, on_device(): pl.pallas_call(functools.partial(gradient_kernel, views), out_shape=(pltp...  4.95 us

profile of v3, /device:TPU:1, one launch (start us, length us, event | category | flops | bytes accessed | tf_op | source)
XLA Modules:
  0.0 39.9 jit_solution(18401344012705218545)
XLA Ops:
  0.6 6.4 %slab.1 = (f32[384,128]{1,0:T(8,128)S(1)}, f32[3,8,128]{2,1,0:T(8,128)S(1)}, f32[2,4,32,8,8,128]{5,4,3,2,1,0:T(8,128)S(1)}) custom-call(s32[4]{0:T(128)} %angle_hbm.1, s32[4]{0:T(128)} %side_hbm.1, f32[4,512,128]{2,1,0:T(8,128)} %bitcast.29, f32[4,512,128]{2,1,0:T(8,128)} %bitcast.30, f32[4,64,128]{2,1,0:T(8,128)} %bitcast.31), custom_call_target="tpu_custom_call" | custom-call | tf_op jit(solution)/shard_map/slab/pallas_call | solution.py:392
  7.1 16.1 %all_to_all.10 = f32[96,4,128]{2,1,0:T(4,128)S(1)} all-to-all(f32[96,4,128]{2,1,0:T(4,128)S(1)} %bitcast.28), channel_id=1, replica_groups=mesh['depth'=8,'rows'=4] {'depth','rows'}, dimensions={0} | all-to-all | bytes 393216 | tf_op jit(solution)/shard_map/all_to_all | solution.py:417
  23.2 0.4 column.1
  23.5 11.4 %all_to_all.11 = f32[96,4,128]{2,1,0:T(4,128)S(1)} all-to-all(f32[96,4,128]{2,1,0:T(4,128)S(1)} %bitcast.26), channel_id=1, replica_groups=mesh['depth'=8,'rows'=4] {'depth','rows'}, dimensions={0} | all-to-all | bytes 393216 | tf_op jit(solution)/shard_map/all_to_all | solution.py:417
  34.9 5.0 %gradient.1 = (f32[4,512,128]{2,1,0:T(8,128)}, f32[4,512,128]{2,1,0:T(8,128)}) custom-call(f32[3,8,128]{2,1,0:T(8,128)S(1)} %get-tuple-element.7.tilt_ref, f32[384,128]{1,0:T(8,128)S(1)} %bitcast.27, f32[2,4,32,8,8,128]{5,4,3,2,1,0:T(8,128)S(1)} %get-tuple-element.9.field_ref), custom_call_target="tpu_custom_call" | custom-call | tf_op jit(solution)/shard_map/gradient/pallas_call | solution.py:448

commit v4 on v3

--- a/solution.py
+++ b/solution.py
@@ -84,6 +84,37 @@
     small = [pltpu.make_async_copy(angle_hbm, angle_ref, sem.at[0]), pltpu.make_async_copy(side_hbm, side_ref, sem.at[1])]
     for copy in small + [copy for b in range(blocks) for copy in fetch(b)]:
         copy.start()
+    scale = -math.log2(math.e)
+    sum_ref[...] = jnp.zeros(sum_ref.shape, F32)
+
+    steps = 8
+
+    def shifts(i, carry):
+        b = i // (SUBS // steps)
+        first = lax.rem(i, SUBS // steps)
+
+        @pl.when(first == 0)
+        def _():
+            for copy in fetch(b):
+                copy.wait()
+
+        sums = [sum_ref[g] for g in range(groups)]
+        for step in range(steps):
+            z, row = i * steps + step, first * steps + step
+            for f, ref in enumerate((ax_ref, dx_ref)):
+                values = [raw_ref[f, b, pl.ds(g * GROUP + row, SUBS, stride=SUBS), :] for g in range(groups)]
+                if f == 0:
+                    values = [scale * x for x in values]
+                    sums = [x + y for x, y in zip(sums, values)]
+                for g, (here, left, right) in enumerate(zip(values, moved_right(values), moved_left(values))):
+                    ref[0, z, g] = here
+                    ref[1, z, g] = left - here
+                    ref[2, z, g] = right - here
+        for g in range(groups):
+            sum_ref[g] = sums[g]
+        return carry
+
+    lax.fori_loop(0, cells // steps, shifts, 0)
     for copy in small:
         copy.wait()
     order = near_first(side_ref, views)
@@ -101,52 +132,31 @@
     beside = parts[1] + parts[2]
     weights = [spread(beside[p : p + 1]) for p in range(views)]
     shift = [jnp.where(leans_right(angle_ref[order[p]]), 0, 1) for p in range(views)]
-    scale = -math.log2(math.e)
-    sum_ref[...] = jnp.zeros(sum_ref.shape, F32)
-
-    def shifts(z, carry):
-        b = z // SUBS
-        row = lax.rem(z, SUBS)
-
-        @pl.when(row == 0)
-        def _():
-            for copy in fetch(b):
-                copy.wait()
-
-        absorbs = [scale * raw_ref[0, b, pl.ds(g * GROUP + row, SUBS, stride=SUBS), :] for g in range(groups)]
-        for g, (here, left, right) in enumerate(zip(absorbs, moved_right(absorbs), moved_left(absorbs))):
-            ax_ref[0, z, g] = here
-            ax_ref[1, z, g] = left - here
-            ax_ref[2, z, g] = right - here
-            sum_ref[g] = sum_ref[g] + here
-        density = [raw_ref[1, b, pl.ds(g * GROUP + row, SUBS, stride=SUBS), :] for g in range(groups)]
-        for g, (here, left, right) in enumerate(zip(density, moved_right(density), moved_left(density))):
-            dx_ref[0, z, g] = here
-            dx_ref[1, z, g] = left - here
-            dx_ref[2, z, g] = right - here
-        return carry
-
-    lax.fori_loop(0, cells, shifts, 0)
 
     def put(g, field, value):
         up_ref[pl.ds(g * SUBS * fields + field, SUBS, stride=fields), :] = value
 
-    def rays(g, carry):
-        depth = [jnp.zeros(TILE, F32)] * views
-        front = [jnp.zeros(TILE, F32)] * views
+    abreast = 2
+
+    def rays(i, carry):
+        several = [i * abreast + j for j in range(abreast)]
+        depth = {(j, p): jnp.zeros(TILE, F32) for j in range(abreast) for p in range(views)}
+        front = dict(depth)
         for i in range(cells):
+            for j, g in enumerate(several):
+                for p in range(views):
+                    z = i if p < views // 2 else cells - 1 - i
+                    light = jnp.exp2(depth[j, p])
+                    depth[j, p] = depth[j, p] + (ax_ref[0, z, g] + weights[p] * ax_ref[1 + shift[p], z, g])
+                    front[j, p] = front[j, p] + (dx_ref[0, z, g] + weights[p] * dx_ref[1 + shift[p], z, g]) * light
+                    field_ref[0, p, z, g] = light
+                    field_ref[1, p, z, g] = front[j, p]
+        for j, g in enumerate(several):
             for p in range(views):
-                z = i if p < views // 2 else cells - 1 - i
-                light = jnp.exp2(depth[p])
-                depth[p] = depth[p] + (ax_ref[0, z, g] + weights[p] * ax_ref[1 + shift[p], z, g])
-                front[p] = front[p] + (dx_ref[0, z, g] + weights[p] * dx_ref[1 + shift[p], z, g]) * light
-                field_ref[0, p, z, g] = light
-                field_ref[1, p, z, g] = front[p]
-        for p in range(views):
-            put(g, p, front[p])
+                put(g, p, front[j, p])
         return carry
 
-    lax.fori_loop(0, groups, rays, 0)
+    lax.fori_loop(0, groups // abreast, rays, 0)
     fetch_m.wait()
     totals = [sum_ref[g] for g in range(groups)]
     odd = lax.rem(subs(), 2) == 1
@@ -319,8 +329,9 @@
         order = [jnp.where(place == p, v, order[p]) for p in range(views)]
 
     def products(ahead):
-        def body(z, carry):
-            b, row = z // SUBS, lax.rem(z, SUBS)
+        steps = 4
+
+        def cell(z, b, row):
             sums = [[], [], [], [], [], []]
             for g in range(groups):
                 for q in range(2):
@@ -340,14 +351,20 @@
                 for g in range(groups):
                     out_ref[q, b, pl.ds(g * GROUP + row, SUBS, stride=SUBS), :] = total[g]
 
-            @pl.when(row == SUBS - 1)
+        def body(i, carry):
+            b = i // (SUBS // steps)
+            first = lax.rem(i, SUBS // steps)
+            for step in range(steps):
+                cell(i * steps + step, b, first * steps + step)
+
+            @pl.when(first == SUBS // steps - 1)
             def _():
                 for copy in send(b):
                     copy.start()
 
             return carry
 
-        lax.fori_loop(0, cells, body, 0)
+        lax.fori_loop(0, cells // steps, body, 0)
 
     for ahead in range(views + 1):
 

time: 40 us -> 35.9 us (0.90)
  Pallas kernels: 11.7 us -> 7.58 us
    pallas_call x1, Pallas kernels: 6.44 us -> 3.83 us  [on_device(): pl.pallas_call(functools.partial(slab_kernel, views, slabs), out_shape=(p...]
    pallas_call x1, Pallas kernels: 4.95 us -> 3.4 us  [on_device(): pl.pallas_call(functools.partial(gradient_kernel, views), out_shape=(pltp...]
where the time goes in v4:
time: 35.9 us; the launch traced here: 35.7 us
  blocking collectives  27.5 us (77%)
  Pallas kernels  7.58 us (21%)
  between operations  0.65 us (2%)
    all_to_all x2, blocking collectives, exchange(): return lax.all_to_all(x, ('depth', 'rows'), 0, 0, tiled=True)  27.5 us
    pallas_call x1, Pallas kernels, on_device(): pl.pallas_call(functools.partial(slab_kernel, views, slabs), out_shape=(p...  3.83 us
    pallas_call x1, Pallas kernels, on_device(): pl.pallas_call(functools.partial(gradient_kernel, views), out_shape=(pltp...  3.4 us

profile of v4, /device:TPU:1, one launch (start us, length us, event | category | flops | bytes accessed | tf_op | source)
XLA Modules:
  0.0 35.7 jit_solution(1236259249056058594)
XLA Ops:
  0.6 3.8 %slab.1 = (f32[384,128]{1,0:T(8,128)S(1)}, f32[3,8,128]{2,1,0:T(8,128)S(1)}, f32[2,4,32,8,8,128]{5,4,3,2,1,0:T(8,128)S(1)}) custom-call(s32[4]{0:T(128)} %angle_hbm.1, s32[4]{0:T(128)} %side_hbm.1, f32[4,512,128]{2,1,0:T(8,128)} %bitcast.29, f32[4,512,128]{2,1,0:T(8,128)} %bitcast.30, f32[4,64,128]{2,1,0:T(8,128)} %bitcast.31), custom_call_target="tpu_custom_call" | custom-call | tf_op jit(solution)/shard_map/slab/pallas_call | solution.py:409
  4.5 16.1 %all_to_all.10 = f32[96,4,128]{2,1,0:T(4,128)S(1)} all-to-all(f32[96,4,128]{2,1,0:T(4,128)S(1)} %bitcast.28), channel_id=1, replica_groups=mesh['depth'=8,'rows'=4] {'depth','rows'}, dimensions={0} | all-to-all | bytes 393216 | tf_op jit(solution)/shard_map/all_to_all | solution.py:434
  20.6 0.4 column.1
  20.9 11.4 %all_to_all.11 = f32[96,4,128]{2,1,0:T(4,128)S(1)} all-to-all(f32[96,4,128]{2,1,0:T(4,128)S(1)} %bitcast.26), channel_id=1, replica_groups=mesh['depth'=8,'rows'=4] {'depth','rows'}, dimensions={0} | all-to-all | bytes 393216 | tf_op jit(solution)/shard_map/all_to_all | solution.py:434
  32.3 3.4 %gradient.1 = (f32[4,512,128]{2,1,0:T(8,128)}, f32[4,512,128]{2,1,0:T(8,128)}) custom-call(f32[3,8,128]{2,1,0:T(8,128)S(1)} %get-tuple-element.7.tilt_ref, f32[384,128]{1,0:T(8,128)S(1)} %bitcast.27, f32[2,4,32,8,8,128]{5,4,3,2,1,0:T(8,128)S(1)} %get-tuple-element.9.field_ref), custom_call_target="tpu_custom_call" | custom-call | tf_op jit(solution)/shard_map/gradient/pallas_call | solution.py:465

commit v5 on v4

--- a/solution.py
+++ b/solution.py
@@ -47,31 +47,25 @@
     return jnp.broadcast_to(row, TILE)
 
 
-def moved_right(blocks):
+def moved_right(blocks, around=False):
     first_lane, first_sub = lanes() == 0, subs() == 0
-    out, carried = [], jnp.zeros(TILE, F32)
-    for x in blocks:
-        rolled = pltpu.roll(x, 1, 1)
-        down = pltpu.roll(rolled, 1, 0)
-        out.append(jnp.where(first_lane, jnp.where(first_sub, carried, down), rolled))
-        carried = down
-    return out
-
-
-def moved_left(blocks):
+    rolled = [pltpu.roll(x, 1, 1) for x in blocks]
+    down = [pltpu.roll(x, 1, 0) for x in rolled]
+    past = [down[-1] if around else jnp.zeros(TILE, F32)] + down[:-1]
+    return [jnp.where(first_lane, jnp.where(first_sub, x, y), z) for x, y, z in zip(past, down, rolled)]
+
+
+def moved_left(blocks, around=False):
     last_lane, last_sub = lanes() == LANES - 1, subs() == SUBS - 1
-    out, carried = [], jnp.zeros(TILE, F32)
-    for x in reversed(blocks):
-        rolled = pltpu.roll(x, LANES - 1, 1)
-        up = pltpu.roll(rolled, SUBS - 1, 0)
-        out.append(jnp.where(last_lane, jnp.where(last_sub, carried, up), rolled))
-        carried = up
-    return out[::-1]
+    rolled = [pltpu.roll(x, LANES - 1, 1) for x in blocks]
+    up = [pltpu.roll(x, SUBS - 1, 0) for x in rolled]
+    later = up[1:] + [up[0] if around else jnp.zeros(TILE, F32)]
+    return [jnp.where(last_lane, jnp.where(last_sub, x, y), z) for x, y, z in zip(later, up, rolled)]
 
 
 def slab_kernel(
     views, slabs, angle_hbm, side_hbm, d_hbm, a_hbm, m_hbm, up_ref, tilt_ref, field_ref,
-    angle_ref, side_ref, raw_ref, ax_ref, dx_ref, sum_ref, m_ref, sem, sem_raw,
+    angle_ref, side_ref, raw_ref, ax_ref, dx_ref, sum_ref, front_ref, m_ref, sem, sem_raw,
 ):
     blocks, length = raw_ref.shape[1:3]
     cells, groups, fields = blocks * SUBS, length // GROUP, views + 2
@@ -85,6 +79,7 @@
     for copy in small + [copy for b in range(blocks) for copy in fetch(b)]:
         copy.start()
     scale = -math.log2(math.e)
+    corner = jnp.logical_and(lanes() == 0, subs() == 0)
     sum_ref[...] = jnp.zeros(sum_ref.shape, F32)
 
     steps = 8
@@ -106,10 +101,13 @@
                 if f == 0:
                     values = [scale * x for x in values]
                     sums = [x + y for x, y in zip(sums, values)]
-                for g, (here, left, right) in enumerate(zip(values, moved_right(values), moved_left(values))):
+                around = moved_right(values, around=True)
+                for g, (here, left) in enumerate(zip(values, around)):
                     ref[0, z, g] = here
-                    ref[1, z, g] = left - here
-                    ref[2, z, g] = right - here
+                    ref[1, z, g] = (jnp.where(corner, 0.0, left) if g == 0 else left) - here
+                here = jnp.where(corner, 0.0, values[0])
+                ref[0, z, groups] = here
+                ref[1, z, groups] = around[0] - here
         for g in range(groups):
             sum_ref[g] = sums[g]
         return carry
@@ -129,9 +127,9 @@
     parts = tilt_parts(angle_block)
     for i, part in enumerate(parts):
         tilt_ref[i] = part
-    beside = parts[1] + parts[2]
-    weights = [spread(beside[p : p + 1]) for p in range(views)]
-    shift = [jnp.where(leans_right(angle_ref[order[p]]), 0, 1) for p in range(views)]
+    before_weight = jnp.where(parts[1] > 0.0, parts[1], parts[0])
+    weights = [spread(before_weight[p : p + 1]) for p in range(views)]
+    right = [leans_right(angle_ref[order[p]]) for p in range(views)]
 
     def put(g, field, value):
         up_ref[pl.ds(g * SUBS * fields + field, SUBS, stride=fields), :] = value
@@ -140,6 +138,7 @@
 
     def rays(i, carry):
         several = [i * abreast + j for j in range(abreast)]
+        places = [[jnp.where(jnp.logical_or(right[p], g > 0), g, groups) for p in range(views)] for g in several]
         depth = {(j, p): jnp.zeros(TILE, F32) for j in range(abreast) for p in range(views)}
         front = dict(depth)
         for i in range(cells):
@@ -147,16 +146,21 @@
                 for p in range(views):
                     z = i if p < views // 2 else cells - 1 - i
                     light = jnp.exp2(depth[j, p])
-                    depth[j, p] = depth[j, p] + (ax_ref[0, z, g] + weights[p] * ax_ref[1 + shift[p], z, g])
-                    front[j, p] = front[j, p] + (dx_ref[0, z, g] + weights[p] * dx_ref[1 + shift[p], z, g]) * light
+                    at = places[j][p]
+                    depth[j, p] = depth[j, p] + (ax_ref[0, z, at] + weights[p] * ax_ref[1, z, at])
+                    front[j, p] = front[j, p] + (dx_ref[0, z, at] + weights[p] * dx_ref[1, z, at]) * light
                     field_ref[0, p, z, g] = light
                     field_ref[1, p, z, g] = front[j, p]
         for j, g in enumerate(several):
             for p in range(views):
-                put(g, p, front[j, p])
+                front_ref[p, g] = front[j, p]
         return carry
 
     lax.fori_loop(0, groups // abreast, rays, 0)
+    for p in range(views):
+        own = [front_ref[p, g] for g in range(groups)]
+        for g, (here, after) in enumerate(zip(own, moved_left(own, around=True))):
+            put(g, p, jnp.where(right[p], here, after))
     fetch_m.wait()
     totals = [sum_ref[g] for g in range(groups)]
     odd = lax.rem(subs(), 2) == 1
@@ -301,12 +305,18 @@
     def get(g, field):
         return down_ref[pl.ds(g * SUBS * fields + field, SUBS, stride=fields), :]
 
+    corner = jnp.logical_and(lanes() == 0, subs() == 0)
     for p in range(views):
         centre, left, right = [spread(tilt_ref[i, p : p + 1]) for i in range(3)]
-        for g in range(groups):
-            back = get(g, p)
-            scale_ref[0, p, g] = centre * back
-            scale_ref[1, p, g] = (left + right) * back
+        leans = left > 0.0
+        own = [get(g, p) for g in range(groups)]
+        for g, (here, before) in enumerate(zip(own, moved_right(own, around=True))):
+            back = jnp.where(leans, here, before)
+            inner, outer = centre * back, (left + right) * back
+            if g == 0:
+                outer = jnp.where(corner, 0.0, outer)
+            scale_ref[0, p, g] = jnp.where(leans, inner, outer)
+            scale_ref[1, p, g] = jnp.where(leans, outer, inner)
     odd = lax.rem(subs(), 2) == 1
     extras = [get(g, views + 1) for g in range(groups)]
     zero = jnp.zeros(TILE, F32)
@@ -319,59 +329,35 @@
         earlier = jnp.where(subs() == 0, past, earlier)
         scale_ref[2, 0, g] = get(g, views) + jnp.where(odd, later, earlier)
 
-    right_of = [(tilt_ref[1, p, 0] > 0.0).astype(jnp.int32) for p in range(views)]
-    count = sum(right_of)
-    order = [0] * views
-    seen = [jnp.int32(0), count]
-    for v in range(views):
-        place = jnp.where(right_of[v] == 1, seen[0], seen[1])
-        seen = [seen[0] + right_of[v], seen[1] + 1 - right_of[v]]
-        order = [jnp.where(place == p, v, order[p]) for p in range(views)]
-
-    def products(ahead):
-        steps = 4
-
-        def cell(z, b, row):
-            sums = [[], [], [], [], [], []]
+    steps = 8
+
+    def cell(z, b, row):
+        for q in range(2):
+            sums = [[], []]
             for g in range(groups):
-                for q in range(2):
-                    parts = [scale_ref[2, 0, g] if q == 1 else None, None, None]
-                    for p in range(views):
-                        value = field_ref[q, order[p], z, g]
-                        for i, scale in ((0, scale_ref[0, order[p], g]), (1 if p < ahead else 2, scale_ref[1, order[p], g])):
-                            parts[i] = scale * value if parts[i] is None else parts[i] + scale * value
-                    for i in range(3):
-                        sums[3 * q + i].append(parts[i])
-            for q in range(2):
-                total = sums[3 * q]
-                if ahead > 0:
-                    total = [x + y for x, y in zip(total, moved_left(sums[3 * q + 1]))]
-                if ahead < views:
-                    total = [x + y for x, y in zip(total, moved_right(sums[3 * q + 2]))]
-                for g in range(groups):
-                    out_ref[q, b, pl.ds(g * GROUP + row, SUBS, stride=SUBS), :] = total[g]
-
-        def body(i, carry):
-            b = i // (SUBS // steps)
-            first = lax.rem(i, SUBS // steps)
-            for step in range(steps):
-                cell(i * steps + step, b, first * steps + step)
-
-            @pl.when(first == SUBS // steps - 1)
-            def _():
-                for copy in send(b):
-                    copy.start()
-
-            return carry
-
-        lax.fori_loop(0, cells // steps, body, 0)
-
-    for ahead in range(views + 1):
-
-        @pl.when(count == ahead)
+                values = [field_ref[q, p, z, g] for p in range(views)]
+                for i in range(2):
+                    terms = [scale_ref[i, p, g] * value for p, value in enumerate(values)]
+                    if q == 1 and i == 0:
+                        terms[0] = terms[0] + scale_ref[2, 0, g]
+                    sums[i].append((terms[0] + terms[1]) + (terms[2] + terms[3]))
+            for g, (here, after) in enumerate(zip(sums[0], moved_left(sums[1], around=True))):
+                out_ref[q, b, pl.ds(g * GROUP + row, SUBS, stride=SUBS), :] = here + after
+
+    def body(i, carry):
+        b = i // (SUBS // steps)
+        first = lax.rem(i, SUBS // steps)
+        for step in range(steps):
+            cell(i * steps + step, b, first * steps + step)
+
+        @pl.when(first == SUBS // steps - 1)
         def _():
-            products(ahead)
-
+            for copy in send(b):
+                copy.start()
+
+        return carry
+
+    lax.fori_loop(0, cells // steps, body, 0)
     for b in range(cells // SUBS):
         for copy in send(b):
             copy.wait()
@@ -405,7 +391,7 @@
     ids_in = [in_hbm(angle_ids), in_hbm(sides)]
     ids = [pltpu.SMEM((views,), jnp.int32)] * 2
     field = pltpu.VMEM((2, views, cells, groups) + TILE, F32)
-    shifted = pltpu.VMEM((3, cells, groups, SUBS, LANES), F32)
+    shifted = pltpu.VMEM((2, cells, groups + 1) + TILE, F32)
     up, tilts, light = pl.pallas_call(
         functools.partial(slab_kernel, views, slabs),
         out_shape=(pltpu.VMEM((tiles * fields, LANES), F32), pltpu.VMEM((3,) + TILE, F32), field),
@@ -417,6 +403,7 @@
             shifted,
             shifted,
             pltpu.VMEM((groups,) + TILE, F32),
+            pltpu.VMEM((views, groups) + TILE, F32),
             pltpu.VMEM((tiles, LANES), F32),
             pltpu.SemaphoreType.DMA((3,)),
             pltpu.SemaphoreType.DMA((2, blocks)),

time: 35.9 us -> 35.5 us (0.989)
  Pallas kernels: 7.58 us -> 7.22 us
where the time goes in v5:
time: 35.5 us; the launch traced here: 35.3 us
  blocking collectives  27.5 us (77%)
  Pallas kernels  7.22 us (20%)
  between operations  0.65 us (2%)
    all_to_all x2, blocking collectives, exchange(): return lax.all_to_all(x, ('depth', 'rows'), 0, 0, tiled=True)  27.5 us
    pallas_call x1, Pallas kernels, on_device(): pl.pallas_call(functools.partial(slab_kernel, views, slabs), out_shape=(p...  3.81 us
    pallas_call x1, Pallas kernels, on_device(): pl.pallas_call(functools.partial(gradient_kernel, views), out_shape=(pltp...  3.06 us

profile of v5, /device:TPU:1, one launch (start us, length us, event | category | flops | bytes accessed | tf_op | source)
XLA Modules:
  0.0 35.3 jit_solution(1816702582718773003)
XLA Ops:
  0.6 3.8 %slab.1 = (f32[384,128]{1,0:T(8,128)S(1)}, f32[3,8,128]{2,1,0:T(8,128)S(1)}, f32[2,4,32,8,8,128]{5,4,3,2,1,0:T(8,128)S(1)}) custom-call(s32[4]{0:T(128)} %angle_hbm.1, s32[4]{0:T(128)} %side_hbm.1, f32[4,512,128]{2,1,0:T(8,128)} %bitcast.29, f32[4,512,128]{2,1,0:T(8,128)} %bitcast.30, f32[4,64,128]{2,1,0:T(8,128)} %bitcast.31), custom_call_target="tpu_custom_call" | custom-call | tf_op jit(solution)/shard_map/slab/pallas_call | solution.py:395
  4.4 16.1 %all_to_all.10 = f32[96,4,128]{2,1,0:T(4,128)S(1)} all-to-all(f32[96,4,128]{2,1,0:T(4,128)S(1)} %bitcast.28), channel_id=1, replica_groups=mesh['depth'=8,'rows'=4] {'depth','rows'}, dimensions={0} | all-to-all | bytes 393216 | tf_op jit(solution)/shard_map/all_to_all | solution.py:421
  20.5 0.4 column.1
  20.9 11.4 %all_to_all.11 = f32[96,4,128]{2,1,0:T(4,128)S(1)} all-to-all(f32[96,4,128]{2,1,0:T(4,128)S(1)} %bitcast.26), channel_id=1, replica_groups=mesh['depth'=8,'rows'=4] {'depth','rows'}, dimensions={0} | all-to-all | bytes 393216 | tf_op jit(solution)/shard_map/all_to_all | solution.py:421
  32.3 3.1 %gradient.1 = (f32[4,512,128]{2,1,0:T(8,128)}, f32[4,512,128]{2,1,0:T(8,128)}) custom-call(f32[3,8,128]{2,1,0:T(8,128)S(1)} %get-tuple-element.7.tilt_ref, f32[384,128]{1,0:T(8,128)S(1)} %bitcast.27, f32[2,4,32,8,8,128]{5,4,3,2,1,0:T(8,128)S(1)} %get-tuple-element.9.field_ref), custom_call_target="tpu_custom_call" | custom-call | tf_op jit(solution)/shard_map/gradient/pallas_call | solution.py:452

commit v6 on v5

--- a/solution.py
+++ b/solution.py
@@ -11,6 +11,7 @@
 ANGLES = 360
 LANES, SUBS = 128, 8
 GROUP = SUBS * SUBS
+ABREAST = 2
 TILE = (SUBS, LANES)
 F32 = jnp.float32
 
@@ -65,54 +66,64 @@
 
 def slab_kernel(
     views, slabs, angle_hbm, side_hbm, d_hbm, a_hbm, m_hbm, up_ref, tilt_ref, field_ref,
-    angle_ref, side_ref, raw_ref, ax_ref, dx_ref, sum_ref, front_ref, m_ref, sem, sem_raw,
+    angle_ref, side_ref, raw_ref, tail_ref, even_ref, odd_ref, last_ref, front_ref, m_ref, sem, sem_raw,
 ):
     blocks, length = raw_ref.shape[1:3]
     cells, groups, fields = blocks * SUBS, length // GROUP, views + 2
     slab = lax.axis_index("depth")
     share = max(slabs // views, 1)
-
-    def fetch(b):
-        return [pltpu.make_async_copy(hbm.at[b], raw_ref.at[f, b], sem_raw.at[f, b]) for f, hbm in enumerate((a_hbm, d_hbm))]
-
+    abreast = even_ref.shape[3] - 1
+    turns = groups // abreast
+    scale = -math.log2(math.e)
+    factors = (scale, 1.0)
+    first_lane, first_sub = lanes() == 0, subs() == 0
+    corner = jnp.logical_and(first_lane, first_sub)
+
+    def fetch(turn):
+        part = pl.ds(turn * abreast * GROUP, abreast * GROUP)
+        return [
+            pltpu.make_async_copy(hbm.at[:, part], raw_ref.at[f, :, part], sem_raw.at[f, turn])
+            for f, hbm in enumerate((a_hbm, d_hbm))
+        ]
+
+    ends = [
+        pltpu.make_async_copy(hbm.at[:, pl.ds(length - SUBS, SUBS)], tail_ref.at[f], sem_raw.at[f, turns])
+        for f, hbm in enumerate((a_hbm, d_hbm))
+    ]
     small = [pltpu.make_async_copy(angle_hbm, angle_ref, sem.at[0]), pltpu.make_async_copy(side_hbm, side_ref, sem.at[1])]
-    for copy in small + [copy for b in range(blocks) for copy in fetch(b)]:
+    for copy in ends + fetch(0) + small + [copy for turn in range(1, turns) for copy in fetch(turn)]:
         copy.start()
-    scale = -math.log2(math.e)
-    corner = jnp.logical_and(lanes() == 0, subs() == 0)
-    sum_ref[...] = jnp.zeros(sum_ref.shape, F32)
-
-    steps = 8
-
-    def shifts(i, carry):
-        b = i // (SUBS // steps)
-        first = lax.rem(i, SUBS // steps)
-
-        @pl.when(first == 0)
-        def _():
-            for copy in fetch(b):
-                copy.wait()
-
-        sums = [sum_ref[g] for g in range(groups)]
-        for step in range(steps):
-            z, row = i * steps + step, first * steps + step
-            for f, ref in enumerate((ax_ref, dx_ref)):
-                values = [raw_ref[f, b, pl.ds(g * GROUP + row, SUBS, stride=SUBS), :] for g in range(groups)]
-                if f == 0:
-                    values = [scale * x for x in values]
-                    sums = [x + y for x, y in zip(sums, values)]
-                around = moved_right(values, around=True)
-                for g, (here, left) in enumerate(zip(values, around)):
-                    ref[0, z, g] = here
-                    ref[1, z, g] = (jnp.where(corner, 0.0, left) if g == 0 else left) - here
-                here = jnp.where(corner, 0.0, values[0])
-                ref[0, z, groups] = here
-                ref[1, z, groups] = around[0] - here
-        for g in range(groups):
-            sum_ref[g] = sums[g]
-        return carry
-
-    lax.fori_loop(0, cells // steps, shifts, 0)
+
+    def shift(turn, ref, f, z, ending=None):
+        b, row = z // SUBS, z % SUBS
+        past = jnp.zeros(TILE, F32) if turn == 0 else last_ref[f, z]
+        for j in range(abreast):
+            here = raw_ref[f, b, pl.ds((turn * abreast + j) * GROUP + row, SUBS, stride=SUBS), :]
+            if f == 0:
+                here = scale * here
+            rolled = pltpu.roll(here, 1, 1)
+            down = pltpu.roll(rolled, 1, 0)
+            ref[f, 0, z, j] = here
+            ref[f, 1, z, j] = jnp.where(first_lane, jnp.where(first_sub, past, down), rolled) - here
+            if turn == 0 and j == 0:
+                inner = jnp.where(corner, 0.0, here)
+                ref[f, 0, z, abreast] = inner
+                ref[f, 1, z, abreast] = jnp.where(first_lane, jnp.where(first_sub, ending, down), rolled) - inner
+            if f == 0:
+                sums[turn * abreast + j] = here if sums[turn * abreast + j] is None else sums[turn * abreast + j] + here
+            past = down
+        if turn + 1 < turns:
+            last_ref[f, z] = past
+
+    sums = [None] * groups
+    for copy in ends + fetch(0):
+        copy.wait()
+    for f in range(2):
+        for b in range(blocks):
+            turned = factors[f] * pltpu.roll(tail_ref[f, b], 1, 1)
+            for row in range(SUBS):
+                shift(0, even_ref, f, b * SUBS + row, spread(turned[row : row + 1]))
+
     for copy in small:
         copy.wait()
     order = near_first(side_ref, views)
@@ -134,42 +145,43 @@
     def put(g, field, value):
         up_ref[pl.ds(g * SUBS * fields + field, SUBS, stride=fields), :] = value
 
-    abreast = 2
-
-    def rays(i, carry):
-        several = [i * abreast + j for j in range(abreast)]
-        places = [[jnp.where(jnp.logical_or(right[p], g > 0), g, groups) for p in range(views)] for g in several]
+    for turn in range(turns):
+        ref, other = (even_ref, odd_ref) if turn % 2 == 0 else (odd_ref, even_ref)
+        if turn + 1 < turns:
+            for copy in fetch(turn + 1):
+                copy.wait()
         depth = {(j, p): jnp.zeros(TILE, F32) for j in range(abreast) for p in range(views)}
         front = dict(depth)
         for i in range(cells):
-            for j, g in enumerate(several):
+            for j in range(abreast):
+                g = turn * abreast + j
                 for p in range(views):
                     z = i if p < views // 2 else cells - 1 - i
+                    at = jnp.where(right[p], 0, abreast) if g == 0 else j
                     light = jnp.exp2(depth[j, p])
-                    at = places[j][p]
-                    depth[j, p] = depth[j, p] + (ax_ref[0, z, at] + weights[p] * ax_ref[1, z, at])
-                    front[j, p] = front[j, p] + (dx_ref[0, z, at] + weights[p] * dx_ref[1, z, at]) * light
+                    depth[j, p] = depth[j, p] + (ref[0, 0, z, at] + weights[p] * ref[0, 1, z, at])
+                    front[j, p] = front[j, p] + (ref[1, 0, z, at] + weights[p] * ref[1, 1, z, at]) * light
                     field_ref[0, p, z, g] = light
                     field_ref[1, p, z, g] = front[j, p]
-        for j, g in enumerate(several):
+            if turn + 1 < turns:
+                for f in range(2):
+                    shift(turn + 1, other, f, i)
+        for j in range(abreast):
             for p in range(views):
-                front_ref[p, g] = front[j, p]
-        return carry
-
-    lax.fori_loop(0, groups // abreast, rays, 0)
+                front_ref[p, turn * abreast + j] = front[j, p]
+
     for p in range(views):
         own = [front_ref[p, g] for g in range(groups)]
         for g, (here, after) in enumerate(zip(own, moved_left(own, around=True))):
             put(g, p, jnp.where(right[p], here, after))
     fetch_m.wait()
-    totals = [sum_ref[g] for g in range(groups)]
     odd = lax.rem(subs(), 2) == 1
     second = lax.rem(slab, share) == 1
-    for g, (before, after) in enumerate(zip(moved_right(totals), moved_left(totals))):
+    for g, (before, after) in enumerate(zip(moved_right(sums), moved_left(sums))):
         counts = m_ref[pl.ds(g * SUBS, SUBS), :]
         counts = jnp.where(second, pltpu.roll(counts, SUBS - 1, 0), counts)
-        edges = jnp.where(lanes() == 0, pltpu.roll(before, 1, 0), after)
-        put(g, views, totals[g])
+        edges = jnp.where(first_lane, pltpu.roll(before, 1, 0), after)
+        put(g, views, sums[g])
         put(g, views + 1, jnp.where(odd, edges, counts))
 
 
@@ -368,7 +380,7 @@
     views = measured.shape[0]
     slabs, rows = lax.axis_size("depth"), lax.axis_size("rows")
     devices = slabs * rows
-    assert views == 4 and slabs % views == 0 and cells % SUBS == 0 and columns % (SUBS * LANES) == 0
+    assert views == 4 and slabs % views == 0 and cells % SUBS == 0 and columns % (ABREAST * SUBS * LANES) == 0
     part = columns // devices
     compact = slabs == SUBS and part == 2 * LANES
     blocks, tiles = cells // SUBS, columns // LANES
@@ -391,7 +403,6 @@
     ids_in = [in_hbm(angle_ids), in_hbm(sides)]
     ids = [pltpu.SMEM((views,), jnp.int32)] * 2
     field = pltpu.VMEM((2, views, cells, groups) + TILE, F32)
-    shifted = pltpu.VMEM((2, cells, groups + 1) + TILE, F32)
     up, tilts, light = pl.pallas_call(
         functools.partial(slab_kernel, views, slabs),
         out_shape=(pltpu.VMEM((tiles * fields, LANES), F32), pltpu.VMEM((3,) + TILE, F32), field),
@@ -400,13 +411,14 @@
         scratch_shapes=ids
         + [
             pltpu.VMEM((2, blocks, length, LANES), F32),
-            shifted,
-            shifted,
-            pltpu.VMEM((groups,) + TILE, F32),
+            pltpu.VMEM((2, blocks) + TILE, F32),
+            pltpu.VMEM((2, 2, cells, ABREAST + 1) + TILE, F32),
+            pltpu.VMEM((2, 2, cells, ABREAST + 1) + TILE, F32),
+            pltpu.VMEM((2, cells) + TILE, F32),
             pltpu.VMEM((views, groups) + TILE, F32),
             pltpu.VMEM((tiles, LANES), F32),
             pltpu.SemaphoreType.DMA((3,)),
-            pltpu.SemaphoreType.DMA((2, blocks)),
+            pltpu.SemaphoreType.DMA((2, groups // ABREAST + 1)),
         ],
         compiler_params=grant(24),
         name="slab",

time: 35.5 us -> 35.3 us (level)
  no operation moved by 1% of the time
where the time goes in v6:
time: 35.3 us; the launch traced here: 35.1 us
  blocking collectives  27.5 us (78%)
  Pallas kernels  6.97 us (20%)
  between operations  0.65 us (2%)
    all_to_all x2, blocking collectives, exchange(): return lax.all_to_all(x, ('depth', 'rows'), 0, 0, tiled=True)  27.5 us
    pallas_call x1, Pallas kernels, on_device(): pl.pallas_call(functools.partial(slab_kernel, views, slabs), out_shape=(p...  3.57 us
    pallas_call x1, Pallas kernels, on_device(): pl.pallas_call(functools.partial(gradient_kernel, views), out_shape=(pltp...  3.06 us

profile of v6, /device:TPU:1, one launch (start us, length us, event | category | flops | bytes accessed | tf_op | source)
XLA Modules:
  0.0 35.1 jit_solution(13938410879416872333)
XLA Ops:
  0.6 3.6 %slab.1 = (f32[384,128]{1,0:T(8,128)S(1)}, f32[3,8,128]{2,1,0:T(8,128)S(1)}, f32[2,4,32,8,8,128]{5,4,3,2,1,0:T(8,128)S(1)}) custom-call(s32[4]{0:T(128)} %angle_hbm.1, s32[4]{0:T(128)} %side_hbm.1, f32[4,512,128]{2,1,0:T(8,128)} %bitcast.29, f32[4,512,128]{2,1,0:T(8,128)} %bitcast.30, f32[4,64,128]{2,1,0:T(8,128)} %bitcast.31), custom_call_target="tpu_custom_call" | custom-call | tf_op jit(solution)/shard_map/slab/pallas_call | solution.py:406
  4.2 16.1 %all_to_all.10 = f32[96,4,128]{2,1,0:T(4,128)S(1)} all-to-all(f32[96,4,128]{2,1,0:T(4,128)S(1)} %bitcast.28), channel_id=1, replica_groups=mesh['depth'=8,'rows'=4] {'depth','rows'}, dimensions={0} | all-to-all | bytes 393216 | tf_op jit(solution)/shard_map/all_to_all | solution.py:433
  20.3 0.4 %column.1 = f32[384,128]{1,0:T(8,128)S(1)} custom-call(f32[3,8,128]{2,1,0:T(8,128)S(1)} %get-tuple-element.7.tilt_ref, f32[384,128]{1,0:T(8,128)S(1)} %bitcast.25), custom_call_target="tpu_custom_call" | custom-call | tf_op jit(solution)/shard_map/column/pallas_call | solution.py:449
  20.7 11.4 %all_to_all.11 = f32[96,4,128]{2,1,0:T(4,128)S(1)} all-to-all(f32[96,4,128]{2,1,0:T(4,128)S(1)} %bitcast.26), channel_id=1, replica_groups=mesh['depth'=8,'rows'=4] {'depth','rows'}, dimensions={0} | all-to-all | bytes 393216 | tf_op jit(solution)/shard_map/all_to_all | solution.py:433
  32.0 3.1 %gradient.1 = (f32[4,512,128]{2,1,0:T(8,128)}, f32[4,512,128]{2,1,0:T(8,128)}) custom-call(f32[3,8,128]{2,1,0:T(8,128)S(1)} %get-tuple-element.7.tilt_ref, f32[384,128]{1,0:T(8,128)S(1)} %bitcast.27, f32[2,4,32,8,8,128]{5,4,3,2,1,0:T(8,128)S(1)} %get-tuple-element.9.field_ref), custom_call_target="tpu_custom_call" | custom-call | tf_op jit(solution)/shard_map/gradient/pallas_call | solution.py:464
